TPU v7x, 128 devices: a whole 4x4x4 slice. The times are simulated.
128 devices in a mesh: grid: 2 (over core), pts: 64 (over z, x, y).
Axes of the slice: x: 4, y: 4, z: 4, core: 2. Of those that a mesh axis runs over, the one named last changes fastest.
Arguments:
- spectrum: float32 [2, 28672, 1152], P('grid', 'pts'), may hold values from 0.1 to 1
- interaction: bfloat16 [1152, 1152], replicated, may hold values from -0.1875 to 0.1875
- comp_speed: float32 [2, 1152], replicated, may hold values from -0.45 to 0.45
- sea_mask: int32 [2, 28672], replicated, may hold values 0 or 1
- stokes_kernel: float32 [1152, 80], replicated, may hold values from -0.1875 to 0.1875
- tile_owner: int32 [2, 28672, 1], P('grid', 'pts'), may hold values from 0 to 63; in each aligned block of 448 rows (0 to 447, 448 to 895, ..., all dimensions but the last counted through in order) at most 14 rows name the same one
- ocean_column: int32 [2, 28672], P('grid', 'pts'), may hold values from 0 to 255
- neighbours: int32 [2, 16384, 4], P('grid', 'pts'), may hold values from 0 to 255
- coriolis: float32 [2, 16384], P('grid', 'pts'), may hold values from -1 to 1
- velocity: float32 [2, 2, 40, 16384], P('grid', None, None, 'pts'), may hold values from -6 to 6
Outputs:
- spectrum_next: float32 [2, 28672, 1152], P('grid', 'pts')
- velocity_next: float32 [2, 2, 40, 16384], P('grid', None, None, 'pts')
Inputs may be any that keep to these rules, and one draw needn't show every extreme that they name: `tile_owner`: at most 14 of the rows of one device name the same tile, and some tile takes exactly 14 of them.
All inputs are finite; a program needn't handle non-finite values.
Results may differ from a plain program's by a relative error of at most 0.0003.
Values sent between devices are 32-bit elements; how exact they have to be, the bound alone decides.
A program may use at most 128 MiB of HBM per device.

v0:
```python
import jax
import jax.numpy as jnp
from jax import lax
from jax.sharding import PartitionSpec as P

GC = 256
SUBSTEPS = 4


def from_partner(value, axis, bit):
    mask = 2**bit
    pairs = [(source, source ^ mask) for source in range(lax.axis_size(axis))]
    return lax.ppermute(value, axis, pairs)


def shift_outer(field, amount):
    length = field.shape[2]
    if amount == 0:
        return field
    if amount > 0:
        padded = jnp.pad(field, ((0, 0), (0, 0), (amount, 0)))
        return padded[:, :, :length]
    padded = jnp.pad(field, ((0, 0), (0, 0), (0, -amount)))
    return padded[:, :, -amount:]


def flat_shift(field, amount):
    inner = field.shape[1]
    outer_step = amount // inner
    remain = amount % inner
    moved = shift_outer(field, outer_step)
    if remain == 0:
        return moved
    carried = shift_outer(field, outer_step + 1)
    return jnp.concatenate([carried[:, inner - remain :], moved[:, : inner - remain]], axis=1)


def advect(field, speed_x, speed_y, mask, not_first, not_last, upper, lower):
    left = flat_shift(field, 1) * not_first
    right = flat_shift(field, -1) * not_last
    sx = speed_x[:, None, None]
    sy = speed_y[:, None, None]
    result = field - jnp.maximum(sx, 0.0) * (field - upper) - jnp.minimum(sx, 0.0) * (lower - field)
    result = result - jnp.maximum(sy, 0.0) * (field - left) - jnp.minimum(sy, 0.0) * (right - field)
    return result * mask


def column_masks(inner, outer):
    flat_index = (
        jnp.arange(outer, dtype=jnp.int32)[None, :] * inner
        + jnp.arange(inner, dtype=jnp.int32)[:, None]
    )
    column = flat_index % GC
    return ((column != 0).astype(jnp.float32), (column != GC - 1).astype(jnp.float32))


def select_columns(flow, chosen):
    columns = flow.shape[1]
    picker = (jnp.arange(columns, dtype=jnp.int32)[:, None] == chosen[None, :]).astype(jnp.float32)
    return jnp.dot(
        flow, picker, precision=lax.Precision.HIGHEST, preferred_element_type=jnp.float32
    )


def per_device(
    spectrum,
    interaction,
    comp_speed,
    sea_mask,
    stokes_kernel,
    tile_owner,
    ocean_column,
    neighbours,
    coriolis,
    velocity,
):
    local = spectrum[0]
    held = local.shape[0]
    comps = local.shape[1]
    mix = jnp.dot(local.astype(jnp.bfloat16), interaction, preferred_element_type=jnp.float32)
    relaxed = local + 0.5 * local * jnp.tanh(mix)
    transposed = relaxed.T
    grid_index = lax.axis_index("grid")
    width = lax.axis_size("pts")
    share = comps // width
    sent = transposed.reshape(width, share, held)
    field = lax.all_to_all(sent, "pts", split_axis=0, concat_axis=2, tiled=True)[0].reshape(
        share, width, held
    )
    grid_mask = lax.dynamic_index_in_dim(sea_mask, grid_index, 0, keepdims=False)
    mask = grid_mask.reshape(held, width).T.astype(jnp.float32)[None]
    not_first, not_last = column_masks(width, held)
    speeds = lax.dynamic_slice_in_dim(comp_speed, lax.axis_index("pts") * share, share, 1)
    depth = -(-GC // width)
    for step in range(SUBSTEPS):
        slabs = jnp.stack([field[:, :, :depth], field[:, :, held - depth :]], axis=1)
        other = from_partner(slabs, "grid", 0)
        empty = jnp.zeros_like(other[:, 0])
        top_slab = jnp.where(grid_index == 1, other[:, 1], empty)
        bottom_slab = jnp.where(grid_index == 0, other[:, 0], empty)
        upper = flat_shift(jnp.concatenate([top_slab, field], axis=2), GC)[:, :, depth:]
        lower = flat_shift(jnp.concatenate([field, bottom_slab], axis=2), -GC)[:, :, :held]
        field = advect(
            field, speeds[0], speeds[1], mask, not_first[None], not_last[None], upper, lower
        )
    dealt = field.reshape(share, width * held)
    returned = lax.all_to_all(dealt[None], "pts", split_axis=2, concat_axis=0, tiled=True)
    spectrum_next = returned.reshape(comps, held).T
    stokes = jnp.dot(
        spectrum_next,
        stokes_kernel,
        precision=lax.Precision.HIGHEST,
        preferred_element_type=jnp.float32,
    )
    tiles = lax.axis_size("pts")
    capacity = 2 * held // tiles
    owner = tile_owner[0, :, 0]
    position = jnp.arange(held, dtype=jnp.int32)
    earlier = (owner[:, None] == owner[None, :]) & (position[None, :] < position[:, None])
    rank = jnp.sum(earlier.astype(jnp.int32), axis=1)
    slot = owner * capacity + rank
    placer = (slot[:, None] == jnp.arange(tiles * capacity, dtype=jnp.int32)[None, :]).astype(
        jnp.float32
    )
    payload = jnp.concatenate([stokes, (ocean_column[0] + 1)[:, None].astype(jnp.float32)], axis=1)
    buffer = jnp.dot(
        placer.T, payload, precision=lax.Precision.HIGHEST, preferred_element_type=jnp.float32
    )
    buffer = buffer.reshape(tiles, capacity, payload.shape[1])
    received = lax.all_to_all(buffer, "pts", split_axis=0, concat_axis=0, tiled=True).reshape(
        tiles * capacity, payload.shape[1]
    )
    columns = coriolis.shape[1]
    target = received[:, -1].astype(jnp.int32) - 1
    onehot = (jnp.arange(columns, dtype=jnp.int32)[:, None] == target[None, :]).astype(jnp.float32)
    drift_sum = jnp.dot(
        onehot,
        received[:, :-1],
        precision=lax.Precision.HIGHEST,
        preferred_element_type=jnp.float32,
    )
    count = jnp.sum(onehot, axis=1)
    drift = (drift_sum / jnp.maximum(count, 1.0)[:, None]).T
    levels = drift.shape[0] // 2
    east_drift = drift[:levels]
    north_drift = drift[levels:]
    near = neighbours[0]
    east_flow = velocity[0, 0]
    north_flow = velocity[0, 1]
    zeta = (
        select_columns(north_flow, near[:, 0])
        - select_columns(north_flow, near[:, 1])
        - (select_columns(east_flow, near[:, 2]) - select_columns(east_flow, near[:, 3]))
    )
    spin = coriolis[0][None, :]
    new_east = east_flow + 0.25 * (spin * north_flow + (spin + zeta) * north_drift)
    new_north = north_flow - 0.25 * (spin * east_flow + (spin + zeta) * east_drift)
    return (spectrum_next[None], jnp.stack([new_east, new_north])[None])


def solution(mesh):
    placed = (
        P("grid", "pts", None),
        P(),
        P(),
        P(),
        P(),
        P("grid", "pts", None),
        P("grid", "pts"),
        P("grid", "pts", None),
        P("grid", "pts"),
        P("grid", None, None, "pts"),
    )
    return jax.shard_map(
        per_device,
        mesh=mesh,
        in_specs=placed,
        out_specs=(P("grid", "pts", None), P("grid", None, None, "pts")),
        check_vma=False,
    )
```

profile of v0, /device:TPU:0, one launch (start us, length us, event | category | flops | bytes accessed | tf_op | source)
XLA Modules:
  0.0 418.4 jit_solution(6501580032724244859)
XLA Ops:
  2.4 5.1 %fusion.54 = f32[1152,448]{0,1:T(8,128)} fusion(bf16[1152,1152]{1,0:T(8,128)(2,1)S(1)} %copy-done, f32[1,448,1152]{2,1,0:T(8,128)} %param.10), kind=kOutput, calls=%fused_computation.79 | convolution fusion | flops 1191149568 | bytes 6782976 | tf_op jit(solution)/shard_map/dot_general | solution.py:80
  11.6 11.6 %all-to-all-start = ((f32[64,18,448]{2,1,0:T(8,128)}), f32[64,18,448]{2,1,0:T(8,128)S(1)}, u32[]{:S(2)}, u32[]{:S(2)}) async-start(f32[64,18,448]{2,1,0:T(8,128)} %reshape.183), calls=%async_computation | async-start | bytes 6291456 | tf_op jit(solution)/shard_map/all_to_all | solution.py:87
  24.7 40.2 %all-to-all-done = f32[64,18,448]{2,1,0:T(8,128)S(1)} async-done(((f32[64,18,448]{2,1,0:T(8,128)}), f32[64,18,448]{2,1,0:T(8,128)S(1)}, u32[]{:S(2)}, u32[]{:S(2)}) %all-to-all-start) | async-done | bytes 2064416 | tf_op jit(solution)/shard_map/all_to_all | solution.py:87
  66.3 3.5 fusion.100
  82.6 5.1 %fusion.32 = f32[18,64,448]{2,0,1:T(8,128)S(1)} fusion(f32[18,64,448]{2,0,1:T(8,128)S(1)} %bitcast.110, f32[18,64,4]{2,0,1:T(8,128)S(1)} %get-tuple-element.54, f32[18,64,4]{2,0,1:T(8,128)S(1)} %get-tuple-element.55, f32[18,63,448]{2,0,1:T(8,128)} %get-tuple-element.29, f32[18,1,448]{2,0,1:T(8,128)} %get-tuple-element.31, f32[18,1,448]{2,0,1:T(8,128)S(1)} %copy-done.9, ...), kind=kLoop, calls=%fused_computation.39 | loop fusion | flops 9805824 | bytes 8638752 | tf_op jit(solution)/shard_map/mul | solution.py:45
  89.3 3.6 fusion.99
  102.8 5.7 %fusion.23 = f32[18,64,448]{2,0,1:T(8,128)S(1)} fusion(f32[18,64,448]{2,0,1:T(8,128)S(1)} %copy-done.3, f32[18,64,4]{2,0,1:T(8,128)S(1)} %select_bitcast_fusion.4, f32[18,64,4]{2,0,1:T(8,128)} %select_bitcast_fusion.5, f32[18,63,448]{2,0,1:T(8,128)} %get-tuple-element.23, f32[18,1,448]{2,0,1:T(8,128)} %get-tuple-element.25, ...), kind=kLoop, calls=%fused_computation.28 | loop fusion | flops 9805824 | bytes 8638752 | tf_op jit(solution)/shard_map/mul | solution.py:45
  108.5 3.7 fusion.98
  116.8 8.0 %fusion.14 = f32[18,64,448]{2,0,1:T(8,128)S(1)} fusion(f32[18,64,448]{2,0,1:T(8,128)} %copy-done.4, f32[18,64,4]{2,0,1:T(8,128)S(1)} %select_bitcast_fusion.2, f32[18,64,4]{2,0,1:T(8,128)} %select_bitcast_fusion.3, f32[18,63,448]{2,0,1:T(8,128)} %get-tuple-element.17, f32[18,1,448]{2,0,1:T(8,128)} %get-tuple-element.19, f32[18,1,448]{2,0,1:T(8,128)} %get-tuple-element.18, ...), kind=kLoop, calls=%fused_computation.17 | loop fusion | flops 9805824 | bytes 8638752 | tf_op jit(solution)/shard_map/mul | solution.py:45
  124.8 3.5 fusion.97
  142.7 6.9 %fusion.5 = f32[18,64,448]{2,0,1:T(8,128)} fusion(f32[18,64,448]{2,0,1:T(8,128)S(1)} %fusion.14, f32[18,64,4]{2,0,1:T(8,128)S(1)} %select_bitcast_fusion, f32[18,64,4]{2,0,1:T(8,128)} %select_bitcast_fusion.1, f32[18,63,448]{2,0,1:T(8,128)} %get-tuple-element.11, f32[18,1,448]{2,0,1:T(8,128)} %get-tuple-element.13, f32[18,1,448]{2,0,1:T(8,128)} %get-tuple-element.12, ...), kind=kLoop, calls=%fused_computation.6 | loop fusion | flops 9805824 | bytes 8638752 | tf_op jit(solution)/shard_map/mul | solution.py:45
  149.7 9.1 %copy.74 = f32[18,64,448]{0,2,1:T(8,128)} copy(f32[18,64,448]{2,0,1:T(8,128)} %fusion.5) | data formatting | bytes 4128768 | tf_op jit(solution)/shard_map/broadcast_in_dim;reshape | solution.py:107
  159.3 128.6 %reduce.6 = f32[28672,18]{1,0:T(8,128)} reduce(f32[28672,1,18]{2,1,0:T(1,128)} %bitcast.111, f32[]{:T(128)} %broadcast.205), dimensions={1}, to_apply=%bitcast.98.reduce_sub_computation | reduce | bytes 4128772
  287.9 16.6 %reshape.195 = f32[64,1,8064]{2,1,0:T(1,128)} reshape(f32[28672,18]{1,0:T(8,128)} %reduce.6) | data formatting | bytes 4128768
  304.4 6.5 %all-to-all-start.1 = ((f32[64,1,8064]{2,1,0:T(1,128)}), f32[64,1,8064]{2,1,0:T(1,128)S(1)}, u32[]{:S(2)}, u32[]{:S(2)}) async-start(f32[64,1,8064]{2,1,0:T(1,128)} %reshape.195), calls=%async_computation.1 | async-start | bytes 4128768 | tf_op jit(solution)/shard_map/all_to_all | solution.py:107
  311.5 29.0 %all-to-all-done.1 = f32[64,1,8064]{2,1,0:T(1,128)S(1)} async-done(((f32[64,1,8064]{2,1,0:T(1,128)}), f32[64,1,8064]{2,1,0:T(1,128)S(1)}, u32[]{:S(2)}, u32[]{:S(2)}) %all-to-all-start.1) | async-done | bytes 2064416 | tf_op jit(solution)/shard_map/all_to_all | solution.py:107
  340.5 7.4 %reduce.7 = f32[64,8064]{1,0:T(8,128)} reduce(f32[64,1,8064]{2,1,0:T(1,128)S(1)} %all-to-all-done.1, f32[]{:T(128)} %broadcast.205), dimensions={1}, to_apply=%all_to_all.28.reduce_sub_computation | reduce | bytes 4128772 | tf_op jit(solution)/shard_map/all_to_all | solution.py:107
  347.9 26.0 %reshape.196 = f32[28672,1,18]{2,1,0:T(1,128)} reshape(f32[64,8064]{1,0:T(8,128)} %reduce.7) | data formatting | bytes 4128768
  373.9 10.0 %copy.75 = f32[1,18,64,448]{3,2,0,1:T(8,128)S(1)} copy(f32[1,18,64,448]{1,3,2,0:T(8,128)} %bitcast.112) | data formatting | bytes 4128768 | tf_op jit(solution)/shard_map/all_to_all | solution.py:107
  383.9 3.0 copy.70
  387.0 2.7 reshape.184
  394.8 6.3 %all-to-all-start.2 = ((f32[64,14,81]{2,1,0:T(8,128)}), f32[64,14,81]{2,1,0:T(8,128)S(1)}, u32[]{:S(2)}, u32[]{:S(2)}) async-start(f32[64,14,81]{2,1,0:T(8,128)} %reshape.185), calls=%async_computation.2 | async-start | bytes 1048576 | tf_op jit(solution)/shard_map/all_to_all | solution.py:130
  401.6 3.1 copy.72
  404.7 8.4 %all-to-all-done.2 = f32[64,14,81]{2,1,0:T(8,128)S(1)} async-done(((f32[64,14,81]{2,1,0:T(8,128)}), f32[64,14,81]{2,1,0:T(8,128)S(1)}, u32[]{:S(2)}, u32[]{:S(2)}) %all-to-all-start.2) | async-done | bytes 290336 | tf_op jit(solution)/shard_map/all_to_all | solution.py:130
  (104 shorter events, 63.3 us)
Async XLA Ops:
  0.6 1.8 copy-start
  11.6 11.7 %copy-start.10 = (s32[2,28672]{1,0:T(2,128)S(1)}, s32[2,28672]{1,0:T(2,128)}, u32[]{:S(2)}) copy-start(s32[2,28672]{1,0:T(2,128)} %param.13) | copy-start | bytes 688132
  11.6 53.2 %all-to-all-start = ((f32[64,18,448]{2,1,0:T(8,128)}), f32[64,18,448]{2,1,0:T(8,128)S(1)}, u32[]{:S(2)}, u32[]{:S(2)}) async-start(f32[64,18,448]{2,1,0:T(8,128)} %reshape.183), calls=%async_computation | async-start | bytes 6291456 | tf_op jit(solution)/shard_map/all_to_all | solution.py:87
  74.6 1.3 collective-permute-start
  80.5 2.1 copy-start.6
  80.5 2.1 copy-start.9
  87.7 1.6 copy-start.2
  93.4 2.3 collective-permute-start.1
  95.8 7.0 %copy-start.3 = (f32[18,64,448]{2,0,1:T(8,128)S(1)}, f32[18,64,448]{2,0,1:T(8,128)}, u32[]{:S(2)}) copy-start(f32[18,64,448]{2,0,1:T(8,128)} %copy-done.2) | copy-start | bytes 6193156
  108.5 3.7 copy-start.4
  113.1 2.0 collective-permute-start.2
  134.5 1.5 collective-permute-start.3
  304.4 6.5 %copy-start.11 = (s32[1,448,1]{1,2,0:T(1,128)S(1)}, s32[1,448,1]{1,2,0:T(1,128)}, u32[]{:S(2)}) copy-start(s32[1,448,1]{1,2,0:T(1,128)} %param.15) | copy-start | bytes 5380
  304.4 6.8 %copy-start.14 = (s32[1,448]{1,0:T(1,128)S(1)}, s32[1,448]{1,0:T(1,128)}, u32[]{:S(2)}) copy-start(s32[1,448]{1,0:T(1,128)} %param.16) | copy-start | bytes 5380
  304.4 6.8 %copy-start.13 = (s32[1,256,4]{1,2,0:T(4,128)S(1)}, s32[1,256,4]{1,2,0:T(4,128)}, u32[]{:S(2)}) copy-start(s32[1,256,4]{1,2,0:T(4,128)} %param.17) | copy-start | bytes 12292
  304.4 6.8 %copy-start.8 = (f32[1,2,40,256]{3,2,1,0:T(8,128)S(1)}, f32[1,2,40,256]{3,2,1,0:T(8,128)}, u32[]{:S(2)}) copy-start(f32[1,2,40,256]{3,2,1,0:T(8,128)} %param.19) | copy-start | bytes 245764
  304.4 36.1 %all-to-all-start.1 = ((f32[64,1,8064]{2,1,0:T(1,128)}), f32[64,1,8064]{2,1,0:T(1,128)S(1)}, u32[]{:S(2)}, u32[]{:S(2)}) async-start(f32[64,1,8064]{2,1,0:T(1,128)} %reshape.195), calls=%async_computation.1 | async-start | bytes 4128768 | tf_op jit(solution)/shard_map/all_to_all | solution.py:107
  387.0 4.1 copy-start.7
  389.6 1.4 copy-start.5
  394.8 18.3 %all-to-all-start.2 = ((f32[64,14,81]{2,1,0:T(8,128)}), f32[64,14,81]{2,1,0:T(8,128)S(1)}, u32[]{:S(2)}, u32[]{:S(2)}) async-start(f32[64,14,81]{2,1,0:T(8,128)} %reshape.185), calls=%async_computation.2 | async-start | bytes 1048576 | tf_op jit(solution)/shard_map/all_to_all | solution.py:130
  401.5 16.4 %copy-start.1 = (bf16[1152,1152]{1,0:T(8,128)(2,1)S(1)}, bf16[1152,1152]{1,0:T(8,128)(2,1)}, u32[]{:S(2)}) copy-start(bf16[1152,1152]{1,0:T(8,128)(2,1)} %param.11) | copy-start | bytes 7962628
  401.5 15.5 %copy-start.12 = (f32[1,256]{1,0:T(1,128)S(1)}, f32[1,256]{1,0:T(1,128)}, u32[]{:S(2)}) copy-start(f32[1,256]{1,0:T(1,128)} %param.18) | copy-start | bytes 3076
where the time goes:
time: 426 us; the launch traced here: 418 us
  other arithmetic  173 us (41%)
  local copies, waits for them, and re-layouts  129 us (30%)
  waiting for transfers between devices  78.5 us (18%)
  starting transfers between devices  26.1 us (6%)
  matrix products  10.4 us (2%)
    unnamed x1, other arithmetic  129 us
    unnamed x34, local copies, waits for them, and re-layouts  51.4 us
    all_to_all x1, waiting for transfers between devices, per_device(): lax.all_to_all(sent, 'pts', split_axis=0, concat_axis=2, tiled=True)[0]  40.2 us
    all_to_all x1, waiting for transfers between devices, per_device(): lax.all_to_all(dealt[None], 'pts', split_axis=2, concat_axis=0, tiled=True)  29 us
    mul x4, other arithmetic, advect(): return result * mask  25.7 us
    slice x4, local copies, waits for them, and re-layouts, flat_shift(): carried[:, inner - remain:]  14.3 us
    all_to_all x2, local copies, waits for them, and re-layouts, per_device(): lax.all_to_all(dealt[None], 'pts', split_axis=2, concat_axis=0, tiled=True)  13.1 us
    another operation x12, local copies, waits for them, and re-layouts, per_device(): slabs = jnp.stack([field[:, :, :depth], field[:, :, held - depth:]], axis=1)  12.3 us
  transfers between devices with their start and end apart: 7, of which 5 were waited for; matrix products, arithmetic and copies ran while one was open for 2% of the time, Pallas kernels for 0%

commit v1 on v0

v1 whole, which is shorter than its diff:
```python
import jax
import jax.numpy as jnp
from jax import lax
from jax.experimental import pallas as pl
from jax.experimental.pallas import tpu as pltpu
from jax.sharding import PartitionSpec as P

MESH = pl.DeviceIdType.MESH
LANES = 128
SUB = 8
SIDE = 4
GC = 256


def wave_kernel(
    spec_hbm,
    inter_hbm,
    speed,
    sea,
    kern,
    out_hbm,
    stokes,
    spec,
    inter,
    half,
    sent,
    own,
    left,
    right,
    wide,
    swept,
    back,
    home,
    final,
    mask_pos,
    mask_neg,
    mask_now,
    load_sem,
    store_sem,
    in_send,
    in_recv,
    halo_send,
    halo_recv,
    edge_send,
    edge_recv,
    out_send,
    out_recv,
):
    chunks = spec.shape[0]
    held = spec.shape[1]
    rows = held // SIDE
    tall = rows + 2 * SIDE
    grid = lax.axis_index("grid")
    place = lax.axis_index("pts")
    y = lax.rem(place, SIDE)
    base = place - y
    block = 16 * y + place // SIDE
    after = lax.rem(block + 1, 64)
    before = lax.rem(block + 63, 64)
    after_dev = SIDE * lax.rem(after, 16) + after // 16
    before_dev = SIDE * lax.rem(before, 16) + before // 16
    peers = [base + lax.rem(y + d, SIDE) for d in (1, 2, 3)]
    lanes = lambda k: pl.ds(pl.multiple_of(k * LANES, LANES), LANES)

    def load(k):
        return (
            pltpu.make_async_copy(spec_hbm.at[:, lanes(k)], spec.at[k], load_sem.at[0, k]),
            pltpu.make_async_copy(inter_hbm.at[:, lanes(k)], inter.at[k], load_sem.at[1, k]),
        )

    @pl.loop(0, chunks)
    def _(k):
        load(k)[0].start()

    @pl.loop(0, chunks)
    def _(k):
        load(k)[1].start()

    barrier = pltpu.get_barrier_semaphore()
    for peer in peers + [after_dev, before_dev]:
        pl.semaphore_signal(barrier, inc=1, device_id={"pts": peer}, device_id_type=MESH)
    pl.semaphore_signal(barrier, inc=1, device_id={"grid": 1 - grid}, device_id_type=MESH)
    pl.semaphore_wait(barrier, 6)

    for k in range(chunks):
        load(k)[0].wait()
        for m in range(SIDE):
            half[m * rows : (m + 1) * rows, k * LANES : (k + 1) * LANES] = spec[
                k, pl.ds(m, rows, stride=SIDE), :
            ].astype(jnp.bfloat16)

    row_at = lax.broadcasted_iota(jnp.int32, (tall, 2 * rows), 0) + (rows * grid - SIDE)
    row_of = lax.broadcasted_iota(jnp.int32, (tall, 2 * rows), 1)
    picked = jnp.dot(
        (row_at == row_of).astype(jnp.bfloat16),
        sea[...].astype(jnp.bfloat16),
        preferred_element_type=jnp.float32,
    ).astype(jnp.bfloat16)
    column = lax.broadcasted_iota(jnp.int32, (GC, LANES), 0)
    for s in range(SUB):
        first = (column == SIDE * block - SIDE + s).astype(jnp.bfloat16)
        second = (column == SIDE * block + 7 - s).astype(jnp.bfloat16)
        mask_pos[pl.ds(s, tall, stride=SUB), :] = jnp.dot(
            picked, first, preferred_element_type=jnp.float32
        )
        mask_neg[pl.ds(s, tall, stride=SUB), :] = jnp.dot(
            picked, second, preferred_element_type=jnp.float32
        )

    def send_in(k, d):
        return pltpu.make_async_remote_copy(
            src_ref=sent.at[k, lax.rem(y + d, SIDE)],
            dst_ref=own.at[k, y],
            send_sem=in_send.at[k, d - 1],
            recv_sem=in_recv.at[k, d - 1],
            device_id={"pts": peers[d - 1]},
            device_id_type=MESH,
        )

    def send_halo(k, side):
        return pltpu.make_async_remote_copy(
            src_ref=own.at[k],
            dst_ref=(left if side == 0 else right).at[k],
            send_sem=halo_send.at[k, side],
            recv_sem=halo_recv.at[k, side],
            device_id={"pts": after_dev if side == 0 else before_dev},
            device_id_type=MESH,
        )

    def send_edge(k):
        at = pl.multiple_of((rows - (rows - SIDE) * grid) * SUB, SUB)
        to = pl.multiple_of((rows + SIDE) * SUB * grid, SUB)
        return pltpu.make_async_remote_copy(
            src_ref=wide.at[k, pl.ds(at, SIDE * SUB)],
            dst_ref=wide.at[k, pl.ds(to, SIDE * SUB)],
            send_sem=edge_send.at[k],
            recv_sem=edge_recv.at[k],
            device_id={"grid": 1 - grid},
            device_id_type=MESH,
        )

    def send_out(k, d):
        return pltpu.make_async_remote_copy(
            src_ref=back.at[k, lax.rem(y + d, SIDE)],
            dst_ref=home.at[k, y],
            send_sem=out_send.at[k, d - 1],
            recv_sem=out_recv.at[k, d - 1],
            device_id={"pts": peers[d - 1]},
            device_id_type=MESH,
        )

    def store(k):
        return pltpu.make_async_copy(final.at[k], out_hbm.at[:, lanes(k)], store_sem.at[k])

    def relax(k):
        load(k)[1].wait()
        mix = jnp.dot(half[...], inter[k], preferred_element_type=jnp.float32)
        grown = jnp.tanh(mix)
        for m in range(SIDE):
            local = spec[k, pl.ds(m, rows, stride=SIDE), :]
            sent[k, m] = local + 0.5 * local * grown[m * rows : (m + 1) * rows]
        own[k, y] = sent[k, y]
        for d in (2, 1, 3):
            send_in(k, d).start()

    def positive(k):
        return speed[1:2, lanes(k)] > 0.0

    def assemble(k):
        pos = jnp.broadcast_to(positive(k), (rows, LANES))
        from_left = block > 0
        from_right = block < 63
        for s in range(SIDE):
            lower = jnp.where(from_left, left[k, s], 0.0)
            upper = jnp.where(from_right, right[k, SIDE - 1 - s], 0.0)
            wide[k, pl.ds(SIDE * SUB + s, rows, stride=SUB), :] = jnp.where(pos, lower, upper)
        for q in range(SIDE):
            wide[k, pl.ds(SIDE * SUB + SIDE + q, rows, stride=SUB), :] = jnp.where(
                pos, own[k, q], own[k, SIDE - 1 - q]
            )
        outside = pl.multiple_of((rows + SIDE) * SUB * grid, SUB)
        wide[k, pl.ds(outside, SIDE * SUB), :] = jnp.zeros((SIDE * SUB, LANES), jnp.float32)

    def sweep(k):
        spread = lambda v: jnp.broadcast_to(v, (SUB, LANES))
        cx = speed[0:1, lanes(k)]
        cy = speed[1:2, lanes(k)]
        down_rate = spread(jnp.maximum(cx, 0.0))
        up_rate = spread(jnp.maximum(-cx, 0.0))
        side_rate = spread(jnp.abs(cy))
        keep = 1.0 - down_rate - up_rate - side_rate
        pos = spread(cy) > 0.0

        @pl.loop(0, tall // SUB)
        def _(part):
            for u in range(SUB):
                at = pl.ds(pl.multiple_of((part * SUB + u) * SUB, SUB), SUB)
                mask_now[at, :] = jnp.where(pos, mask_pos[at, :], mask_neg[at, :])

        zero = jnp.zeros((SUB, LANES), jnp.float32)

        def part(i, carry):
            held_rows = [list(pair) for pair in carry[0]]
            masks = list(carry[1])
            for u in range(SUB):
                at = pl.ds(pl.multiple_of((i * SUB + u) * SUB, SUB), SUB)
                value = wide[k, at, :]
                for stage in range(SIDE):
                    previous, current = held_rows[stage]
                    moved = (
                        keep * current
                        + down_rate * previous
                        + up_rate * value
                        + side_rate * pltpu.roll(current, 1, 0)
                    )
                    held_rows[stage] = [current, value]
                    value = moved * masks[stage]
                swept[at, :] = value
                masks = [mask_now[at, :]] + masks[: SIDE - 1]
            return tuple(tuple(pair) for pair in held_rows), tuple(masks)

        start = (tuple((zero, zero) for _ in range(SIDE)), (zero,) * SIDE)
        lax.fori_loop(0, tall // SUB, part, start)
        wanted = jnp.broadcast_to(cy > 0.0, (rows, LANES))
        columns = [
            swept[pl.ds(2 * SIDE * SUB + SIDE + q, rows, stride=SUB), :] for q in range(SIDE)
        ]
        for c in range(SIDE):
            back[k, c] = jnp.where(wanted, columns[c], columns[SIDE - 1 - c])
        home[k, y] = back[k, y]
        for d in (2, 1, 3):
            send_out(k, d).start()

    def finish(k):
        for m in range(SIDE):
            final[k, pl.ds(m, rows, stride=SIDE), :] = home[k, m]
        store(k).start()
        stokes[...] += jnp.dot(
            final[k],
            kern[k],
            precision=lax.Precision.HIGHEST,
            preferred_element_type=jnp.float32,
        )

    stokes[...] = jnp.zeros_like(stokes)
    ahead = 2
    for k in range(ahead):
        relax(k)

    @pl.loop(0, chunks + 3)
    def _(t):
        @pl.when(t + ahead < chunks)
        def _():
            relax(t + ahead)

        @pl.when(t < chunks)
        def _():
            for d in (1, 2, 3):
                send_in(t, d).wait_recv()
            for side in range(2):
                send_halo(t, side).start()

        @pl.when((t >= 1) & (t < chunks + 1))
        def _():
            k = t - 1
            for side in range(2):
                send_halo(k, side).wait_recv()
            assemble(k)
            send_edge(k).start()

        @pl.when((t >= 2) & (t < chunks + 2))
        def _():
            k = t - 2
            send_edge(k).wait_recv()
            sweep(k)

        @pl.when(t >= 3)
        def _():
            k = t - 3
            for d in (1, 2, 3):
                send_out(k, d).wait_recv()
            finish(k)

    @pl.loop(0, chunks)
    def _(k):
        for d in (1, 2, 3):
            send_in(k, d).wait_send()
            send_out(k, d).wait_send()
        for side in range(2):
            send_halo(k, side).wait_send()
        send_edge(k).wait_send()
        store(k).wait()


def wave_step(spectrum, interaction, comp_speed, sea, stokes_kernel):
    held, comps = spectrum.shape
    chunks = comps // LANES
    rows = held // SIDE
    tall = rows + 2 * SIDE
    f32 = jnp.float32
    piece = pltpu.VMEM((chunks, SIDE, rows, LANES), f32)
    vmem = pl.BlockSpec(memory_space=pltpu.VMEM)
    anywhere = pl.BlockSpec(memory_space=pl.ANY)
    dma = pltpu.SemaphoreType.DMA
    return pl.pallas_call(
        wave_kernel,
        out_shape=(
            jax.ShapeDtypeStruct((held, comps), f32),
            jax.ShapeDtypeStruct((held, LANES), f32),
        ),
        in_specs=[anywhere, anywhere, vmem, vmem, vmem],
        out_specs=(anywhere, vmem),
        scratch_shapes=[
            pltpu.VMEM((chunks, held, LANES), f32),
            pltpu.VMEM((chunks, comps, LANES), jnp.bfloat16),
            pltpu.VMEM((held, comps), jnp.bfloat16),
            piece,
            piece,
            piece,
            piece,
            pltpu.VMEM((chunks, tall * SUB, LANES), f32),
            pltpu.VMEM((tall * SUB, LANES), f32),
            piece,
            piece,
            pltpu.VMEM((chunks, held, LANES), f32),
            pltpu.VMEM((tall * SUB, LANES), f32),
            pltpu.VMEM((tall * SUB, LANES), f32),
            pltpu.VMEM((tall * SUB, LANES), f32),
            dma((2, chunks)),
            dma((chunks,)),
            dma((chunks, 3)),
            dma((chunks, 3)),
            dma((chunks, 2)),
            dma((chunks, 2)),
            dma((chunks,)),
            dma((chunks,)),
            dma((chunks, 3)),
            dma((chunks, 3)),
        ],
        compiler_params=pltpu.CompilerParams(
            collective_id=0, has_side_effects=True, vmem_limit_bytes=56 << 20
        ),
        name="wave_step",
    )(spectrum, interaction, comp_speed, sea, stokes_kernel)


def select_columns(flow, chosen):
    columns = flow.shape[1]
    picker = (jnp.arange(columns, dtype=jnp.int32)[:, None] == chosen[None, :]).astype(jnp.float32)
    return jnp.dot(
        flow, picker, precision=lax.Precision.HIGHEST, preferred_element_type=jnp.float32
    )


def per_device(
    spectrum,
    interaction,
    comp_speed,
    sea_mask,
    stokes_kernel,
    tile_owner,
    ocean_column,
    neighbours,
    coriolis,
    velocity,
):
    local = spectrum[0]
    held, comps = local.shape
    sea = sea_mask.reshape(-1, GC)
    wide_kernel = jnp.pad(stokes_kernel, ((0, 0), (0, LANES - stokes_kernel.shape[1])))
    spectrum_next, stokes = wave_step(
        local, interaction, comp_speed, sea, wide_kernel.reshape(-1, LANES, LANES)
    )
    stokes = stokes[:, : stokes_kernel.shape[1]]
    tiles = lax.axis_size("pts")
    capacity = 2 * held // tiles
    owner = tile_owner[0, :, 0]
    position = jnp.arange(held, dtype=jnp.int32)
    earlier = (owner[:, None] == owner[None, :]) & (position[None, :] < position[:, None])
    rank = jnp.sum(earlier.astype(jnp.int32), axis=1)
    slot = owner * capacity + rank
    placer = (slot[:, None] == jnp.arange(tiles * capacity, dtype=jnp.int32)[None, :]).astype(
        jnp.float32
    )
    payload = jnp.concatenate([stokes, (ocean_column[0] + 1)[:, None].astype(jnp.float32)], axis=1)
    buffer = jnp.dot(
        placer.T, payload, precision=lax.Precision.HIGHEST, preferred_element_type=jnp.float32
    )
    buffer = buffer.reshape(tiles, capacity, payload.shape[1])
    received = lax.all_to_all(buffer, "pts", split_axis=0, concat_axis=0, tiled=True).reshape(
        tiles * capacity, payload.shape[1]
    )
    columns = coriolis.shape[1]
    target = received[:, -1].astype(jnp.int32) - 1
    onehot = (jnp.arange(columns, dtype=jnp.int32)[:, None] == target[None, :]).astype(jnp.float32)
    drift_sum = jnp.dot(
        onehot,
        received[:, :-1],
        precision=lax.Precision.HIGHEST,
        preferred_element_type=jnp.float32,
    )
    count = jnp.sum(onehot, axis=1)
    drift = (drift_sum / jnp.maximum(count, 1.0)[:, None]).T
    levels = drift.shape[0] // 2
    east_drift = drift[:levels]
    north_drift = drift[levels:]
    near = neighbours[0]
    east_flow = velocity[0, 0]
    north_flow = velocity[0, 1]
    zeta = (
        select_columns(north_flow, near[:, 0])
        - select_columns(north_flow, near[:, 1])
        - (select_columns(east_flow, near[:, 2]) - select_columns(east_flow, near[:, 3]))
    )
    spin = coriolis[0][None, :]
    new_east = east_flow + 0.25 * (spin * north_flow + (spin + zeta) * north_drift)
    new_north = north_flow - 0.25 * (spin * east_flow + (spin + zeta) * east_drift)
    return (spectrum_next[None], jnp.stack([new_east, new_north])[None])


def solution(mesh):
    placed = (
        P("grid", "pts", None),
        P(),
        P(),
        P(),
        P(),
        P("grid", "pts", None),
        P("grid", "pts"),
        P("grid", "pts", None),
        P("grid", "pts"),
        P("grid", None, None, "pts"),
    )
    return jax.shard_map(
        per_device,
        mesh=mesh,
        in_specs=placed,
        out_specs=(P("grid", "pts", None), P("grid", None, None, "pts")),
        check_vma=False,
    )
```

time: 426 us -> 143 us (0.34); the launches traced: 418 us -> 142 us
  other arithmetic: 173 us -> 3.54 us
  local copies, waits for them, and re-layouts: 129 us -> 6.29 us
  Pallas kernels: 0 us -> 104 us
  waiting for transfers between devices: 78.5 us -> 12.4 us
  starting transfers between devices: 26.1 us -> 11.3 us
  matrix products: 10.4 us -> 4.16 us
    unnamed x1 -> x0, other arithmetic: 129 us -> none
    pallas_call x0 -> x1, Pallas kernels: none -> 104 us  [wave_step(): pl.pallas_call(wave_kernel, out_shape=(jax.ShapeDtypeStruct((held, comps)...]
    all_to_all x2 -> x0, waiting for transfers between devices: 69.2 us -> none  [the longest x1 40.2 us: per_device(): lax.all_to_all(sent, 'pts', split_axis=0, concat_axis=2, tiled=True)[0]]
    unnamed x34 -> x10, local copies, waits for them, and re-layouts: 51.4 us -> 2.55 us
    slice x20 -> x0, local copies, waits for them, and re-layouts: 33.6 us -> none  [the longest x4 14.3 us: flat_shift(): carried[:, inner - remain:]]
    mul x5 -> x0, other arithmetic: 25.7 us -> none  [the longest x4 25.7 us: advect(): return result * mask]
    another operation x13 -> x0, local copies, waits for them, and re-layouts: 21.5 us -> none  [the longest x12 12.3 us: per_device(): slabs = jnp.stack([field[:, :, :depth], field[:, :, held - depth:]], axis=1)]
    all_to_all x2 -> x0, starting transfers between devices: 18.1 us -> none  [the longest x1 11.6 us: per_device(): lax.all_to_all(sent, 'pts', split_axis=0, concat_axis=2, tiled=True)[0]]
  transfers between devices with their start and end apart: 7 -> 1, of which waited for: 5 -> 1; matrix products, arithmetic and copies ran while one was open for 2% -> 0% of each run, Pallas kernels for 0% -> 0%
where the time goes in v1:
time: 143 us; the launch traced here: 142 us
  Pallas kernels  104 us (73%)
  waiting for transfers between devices  12.4 us (9%)
  starting transfers between devices  11.3 us (8%)
  local copies, waits for them, and re-layouts  6.29 us (4%)
  matrix products  4.16 us (3%)
  other arithmetic  3.54 us (2%)
    pallas_call x1, Pallas kernels, wave_step(): pl.pallas_call(wave_kernel, out_shape=(jax.ShapeDtypeStruct((held, comps)...  104 us
    all_to_all x1, waiting for transfers between devices, per_device(): lax.all_to_all(buffer, 'pts', split_axis=0, concat_axis=0, tiled=True)  12.4 us
    all_to_all x1, starting transfers between devices, per_device(): lax.all_to_all(buffer, 'pts', split_axis=0, concat_axis=0, tiled=True)  11.3 us
  transfers between devices with their start and end apart: 1, of which 1 were waited for; matrix products, arithmetic and copies ran while one was open for 0% of the time, Pallas kernels for 0%

profile of v1, /device:TPU:0, one launch (start us, length us, event | category | flops | bytes accessed | tf_op | source)
XLA Modules:
  0.0 142.5 jit_solution(3290501151418331862)
XLA Ops:
  0.6 1.0 convert_reduce_fusion.1
  1.6 0.7 multiply_add_fusion
  2.3 1.2 copy.23
  3.5 1.9 %reshape.59.sea = s32[224,256]{1,0:T(8,128)} reshape(s32[2,28672]{1,0:T(2,128)} %param.13) | data formatting | bytes 458752 | tf_op jit(solution)/shard_map/reshape | solution.py:369
  5.4 0.7 convert_bitcast_fusion
  6.1 0.1 copy.20
  6.2 0.9 pad.4.clone
  7.1 104.1 %wave_step.1 = (f32[448,1152]{1,0:T(8,128)}, f32[448,128]{1,0:T(8,128)}) custom-call(f32[448,1152]{1,0:T(8,128)} %bitcast.44, bf16[1152,1152]{1,0:T(8,128)(2,1)} %inter_hbm.1, f32[2,1152]{1,0:T(2,128)} %speed.1, s32[224,256]{1,0:T(8,128)} %reshape.59.sea, f32[9,128,128]{2,1,0:T(8,128)} %bitcast.43), custom_call_target="tpu_custom_call" | custom-call | tf_op jit(solution)/shard_map/wave_step/pallas_call | solution.py:305
  111.2 0.0 copy-start.3
  111.2 0.0 copy-start.1
  111.2 2.7 %fusion = f32[896,81]{1,0:T(8,128)S(1)} fusion(s32[448]{0:T(512)S(1)} %multiply_add_fusion, f32[448,1]{1,0:T(8,128)S(1)} %copy.20, f32[448,80]{1,0:T(8,128)} %bitcast.46), kind=kOutput, calls=%fused_computation.1 | convolution fusion | flops 390606272 | bytes 437248 | tf_op jit(solution)/shard_map/dot_general | solution.py:386
  113.9 0.0 copy-start.2
  113.9 0.8 reshape.61
  114.8 11.3 %all-to-all-start = ((f32[64,14,81]{2,1,0:T(8,128)}), f32[64,14,81]{2,1,0:T(8,128)S(1)}, u32[]{:S(2)}, u32[]{:S(2)}) async-start(f32[64,14,81]{2,1,0:T(8,128)} %reshape.61), calls=%async_computation | async-start | bytes 1048576 | tf_op jit(solution)/shard_map/all_to_all | solution.py:390
  126.1 0.2 fusion.10
  126.3 0.2 fusion.11
  126.5 0.2 convolution_subtract_fusion.1
  126.8 12.4 %all-to-all-done = f32[64,14,81]{2,1,0:T(8,128)S(1)} async-done(((f32[64,14,81]{2,1,0:T(8,128)}), f32[64,14,81]{2,1,0:T(8,128)S(1)}, u32[]{:S(2)}, u32[]{:S(2)}) %all-to-all-start) | async-done | bytes 290336 | tf_op jit(solution)/shard_map/all_to_all | solution.py:390
  139.2 0.3 fusion.7
  139.5 0.2 convert_reduce_fusion
  139.7 0.6 convolution_divide_fusion
  140.3 0.2 fusion.26
  140.5 0.6 maximum_bitcast_fusion
  141.2 1.3 copy.25
  (8 shorter events, 0.1 us)
Async XLA Ops:
  111.2 14.9 %copy-start.3 = (s32[1,256,4]{1,2,0:T(4,128)S(1)}, s32[1,256,4]{1,2,0:T(4,128)}, u32[]{:S(2)}) copy-start(s32[1,256,4]{1,2,0:T(4,128)} %param.17) | copy-start | bytes 12292
  111.2 14.9 %copy-start.1 = (f32[1,2,40,256]{3,2,1,0:T(8,128)S(1)}, f32[1,2,40,256]{3,2,1,0:T(8,128)}, u32[]{:S(2)}) copy-start(f32[1,2,40,256]{3,2,1,0:T(8,128)} %param.19) | copy-start | bytes 245764
  113.9 26.4 %copy-start.2 = (f32[1,256]{1,0:T(1,128)S(1)}, f32[1,256]{1,0:T(1,128)}, u32[]{:S(2)}) copy-start(f32[1,256]{1,0:T(1,128)} %param.18) | copy-start | bytes 3076
  114.8 26.4 %copy-start = (f32[448,1152]{1,0:T(8,128)S(1)}, f32[448,1152]{1,0:T(8,128)}, u32[]{:S(2)}) copy-start(f32[448,1152]{1,0:T(8,128)} %get-tuple-element.4) | copy-start | bytes 6193156
  114.8 24.4 %all-to-all-start = ((f32[64,14,81]{2,1,0:T(8,128)}), f32[64,14,81]{2,1,0:T(8,128)S(1)}, u32[]{:S(2)}, u32[]{:S(2)}) async-start(f32[64,14,81]{2,1,0:T(8,128)} %reshape.61), calls=%async_computation | async-start | bytes 1048576 | tf_op jit(solution)/shard_map/all_to_all | solution.py:390

commit v2 on v1

v2 whole, which is shorter than its diff:
```python
import jax
import jax.numpy as jnp
from jax import lax
from jax.experimental import pallas as pl
from jax.experimental.pallas import tpu as pltpu
from jax.sharding import PartitionSpec as P

MESH = pl.DeviceIdType.MESH
LANES = 128
SUB = 8
SIDE = 4
GC = 256


def wave_kernel(
    spec_hbm,
    inter_hbm,
    speed,
    sea,
    kern,
    owner,
    ocean,
    near,
    coriolis,
    velocity,
    out_hbm,
    velocity_out,
    spec,
    inter,
    half,
    sent,
    own,
    left,
    right,
    wide,
    swept,
    back,
    home,
    final,
    mask_pos,
    mask_neg,
    mask_now,
    sea_rows,
    drift_kernel,
    stokes,
    placer,
    zeta,
    posted,
    arrived,
    load_sem,
    store_sem,
    in_send,
    in_recv,
    halo_send,
    halo_recv,
    edge_send,
    edge_recv,
    out_send,
    out_recv,
    post_send,
    post_recv,
):
    f32, bf16, i32 = jnp.float32, jnp.bfloat16, jnp.int32
    chunks, held = spec.shape[:2]
    rows = held // SIDE
    tall = rows + 2 * SIDE
    tiles, slots = arrived.shape[:2]
    drifts = kern.shape[1]
    levels = drifts // 2
    cols = coriolis.shape[1]
    grid = lax.axis_index("grid")
    place = lax.axis_index("pts")
    y = lax.rem(place, SIDE)
    base = place - y
    block = 16 * y + place // SIDE
    after = lax.rem(block + 1, 64)
    before = lax.rem(block + 63, 64)
    after_dev = SIDE * lax.rem(after, 16) + after // 16
    before_dev = SIDE * lax.rem(before, 16) + before // 16
    peers = [base + lax.rem(y + d, SIDE) for d in (1, 2, 3)]
    lanes = lambda k: pl.ds(pl.multiple_of(k * LANES, LANES), LANES)

    def load_spec(k):
        return pltpu.make_async_copy(spec_hbm.at[:, lanes(k)], spec.at[k], load_sem.at[0, k])

    def load_inter(k):
        return pltpu.make_async_copy(inter_hbm.at[:, lanes(k)], inter.at[k], load_sem.at[1, k])

    barrier = pltpu.get_barrier_semaphore()

    @pl.loop(1, tiles)
    def _(d):
        pl.semaphore_signal(
            barrier, inc=1, device_id={"pts": lax.rem(place + d, tiles)}, device_id_type=MESH
        )

    pl.semaphore_signal(barrier, inc=1, device_id={"grid": 1 - grid}, device_id_type=MESH)

    @pl.loop(0, chunks)
    def _(k):
        load_spec(k).start()

    @pl.loop(0, chunks)
    def _(k):
        load_inter(k).start()

    for k in range(chunks):
        load_spec(k).wait()
        for m in range(SIDE):
            half[m * rows : (m + 1) * rows, k * LANES : (k + 1) * LANES] = spec[
                k, pl.ds(m, rows, stride=SIDE), :
            ].astype(bf16)

    def send_in(k, d):
        return pltpu.make_async_remote_copy(
            src_ref=sent.at[k, lax.rem(y + d, SIDE)],
            dst_ref=own.at[k, y],
            send_sem=in_send.at[k, d - 1],
            recv_sem=in_recv.at[k, d - 1],
            device_id={"pts": peers[d - 1]},
            device_id_type=MESH,
        )

    def send_halo(k, side):
        return pltpu.make_async_remote_copy(
            src_ref=own.at[k],
            dst_ref=(left if side == 0 else right).at[k],
            send_sem=halo_send.at[k, side],
            recv_sem=halo_recv.at[k, side],
            device_id={"pts": after_dev if side == 0 else before_dev},
            device_id_type=MESH,
        )

    def send_edge(k):
        at = pl.multiple_of((rows - (rows - SIDE) * grid) * SUB, SUB)
        to = pl.multiple_of((rows + SIDE) * SUB * grid, SUB)
        return pltpu.make_async_remote_copy(
            src_ref=wide.at[k, pl.ds(at, SIDE * SUB)],
            dst_ref=wide.at[k, pl.ds(to, SIDE * SUB)],
            send_sem=edge_send.at[k],
            recv_sem=edge_recv.at[k],
            device_id={"grid": 1 - grid},
            device_id_type=MESH,
        )

    def send_out(k, d):
        return pltpu.make_async_remote_copy(
            src_ref=back.at[k, lax.rem(y + d, SIDE)],
            dst_ref=home.at[k, y],
            send_sem=out_send.at[k, d - 1],
            recv_sem=out_recv.at[k, d - 1],
            device_id={"pts": peers[d - 1]},
            device_id_type=MESH,
        )

    def post(d):
        peer = lax.rem(place + d, tiles)
        return pltpu.make_async_remote_copy(
            src_ref=posted.at[peer],
            dst_ref=arrived.at[place],
            send_sem=post_send,
            recv_sem=post_recv,
            device_id={"pts": peer},
            device_id_type=MESH,
        )

    def store(k):
        return pltpu.make_async_copy(final.at[k], out_hbm.at[:, lanes(k)], store_sem.at[k])

    def relax(k):
        load_inter(k).wait()
        mix = jnp.dot(half[...], inter[k], preferred_element_type=f32)
        grown = jnp.tanh(mix)
        for m in range(SIDE):
            local = spec[k, pl.ds(m, rows, stride=SIDE), :]
            sent[k, m] = local + 0.5 * local * grown[m * rows : (m + 1) * rows]
        own[k, y] = sent[k, y]

    def launch(k):
        for d in (2, 1, 3):
            send_in(k, d).start()

    def forward(k):
        for d in (1, 2, 3):
            send_in(k, d).wait_recv()
        for side in range(2):
            send_halo(k, side).start()

    def prepare_masks():
        @pl.loop(0, rows)
        def _(r):
            pair = sea[:, pl.ds(pl.multiple_of(r * GC, GC), GC)].astype(f32)
            sea_rows[pl.ds(r, 1), :] = pair[0:1]
            sea_rows[pl.ds(r + rows, 1), :] = pair[1:2]

        row_at = lax.broadcasted_iota(i32, (tall, 2 * rows), 0) + (rows * grid - SIDE)
        row_of = lax.broadcasted_iota(i32, (tall, 2 * rows), 1)
        picked = jnp.dot(
            (row_at == row_of).astype(bf16),
            sea_rows[...].astype(bf16),
            preferred_element_type=f32,
        ).astype(bf16)
        column = lax.broadcasted_iota(i32, (GC, LANES), 0)
        for s in range(SUB):
            first = (column == SIDE * block - SIDE + s).astype(bf16)
            second = (column == SIDE * block + 7 - s).astype(bf16)
            mask_pos[pl.ds(s, tall, stride=SUB), :] = jnp.dot(
                picked, first, preferred_element_type=f32
            )
            mask_neg[pl.ds(s, tall, stride=SUB), :] = jnp.dot(
                picked, second, preferred_element_type=f32
            )

    def split(value):
        high = value.astype(bf16)
        return high, (value - high.astype(f32)).astype(bf16)

    def prepare_kernel():
        drift_kernel[...] = jnp.zeros_like(drift_kernel)
        for k in range(chunks):
            high, low = split(kern[k * LANES : (k + 1) * LANES, :])
            drift_kernel[k, 0:LANES, 0:drifts] = high
            drift_kernel[k, 0:LANES, LANES : LANES + drifts] = low
            drift_kernel[k, LANES : 2 * LANES, 0:drifts] = high

    def prepare_slots():
        down = lax.broadcasted_iota(i32, (held, held), 0)
        across = lax.broadcasted_iota(i32, (held, held), 1)
        owners = jnp.broadcast_to(owner[...].astype(f32), (held, held))
        owner_row = jnp.sum(jnp.where(down == across, owners, 0.0), axis=0, keepdims=True)
        earlier = (owners == owner_row) & (down < across)
        rank = jnp.sum(jnp.where(earlier, 1.0, 0.0), axis=0, keepdims=True)
        slot = owner_row * slots + rank
        for part in range(tiles * slots // LANES):
            at = lax.broadcasted_iota(i32, (LANES, held), 0) + part * LANES
            placer[part * LANES : (part + 1) * LANES, :] = (at.astype(f32) == slot).astype(bf16)
        wanted = jnp.broadcast_to(ocean[...].astype(f32) + 1.0, (held, held))
        target = jnp.sum(jnp.where(down == across, wanted, 0.0), axis=1, keepdims=True)
        lane = lax.broadcasted_iota(i32, (held, LANES), 1)
        stokes[...] = jnp.where(lane == drifts, target, jnp.where(lane == drifts + 1, 1.0, 0.0))

    def prepare_zeta():
        column = lax.broadcasted_iota(i32, (cols, cols), 1)

        def apart(first, second):
            one = (near[:, first : first + 1] == column).astype(f32)
            two = (near[:, second : second + 1] == column).astype(f32)
            return (one - two).astype(bf16)

        def taken(flow, picker):
            high, low = split(flow)
            rest = (flow - high.astype(f32) - low.astype(f32)).astype(bf16)
            total = jnp.zeros(flow.shape, f32)
            for each in (high, low, rest):
                total += lax.dot_general(
                    each, picker, (((1,), (1,)), ((), ())), preferred_element_type=f32
                )
            return total

        zeta[...] = taken(velocity[1], apart(0, 1)) - taken(velocity[0], apart(2, 3))

    def assemble(k):
        pos = jnp.broadcast_to(speed[1:2, lanes(k)] > 0.0, (rows, LANES))
        from_left = block > 0
        from_right = block < 63
        for s in range(SIDE):
            lower = jnp.where(from_left, left[k, s], 0.0)
            upper = jnp.where(from_right, right[k, SIDE - 1 - s], 0.0)
            wide[k, pl.ds(SIDE * SUB + s, rows, stride=SUB), :] = jnp.where(pos, lower, upper)
        for q in range(SIDE):
            wide[k, pl.ds(SIDE * SUB + SIDE + q, rows, stride=SUB), :] = jnp.where(
                pos, own[k, q], own[k, SIDE - 1 - q]
            )
        outside = pl.multiple_of((rows + SIDE) * SUB * grid, SUB)
        wide[k, pl.ds(outside, SIDE * SUB), :] = jnp.zeros((SIDE * SUB, LANES), f32)

    def sweep(k):
        spread = lambda v: jnp.broadcast_to(v, (SUB, LANES))
        cx = speed[0:1, lanes(k)]
        cy = speed[1:2, lanes(k)]
        down_rate = spread(jnp.maximum(cx, 0.0))
        up_rate = spread(jnp.maximum(-cx, 0.0))
        side_rate = spread(jnp.abs(cy))
        keep = 1.0 - down_rate - up_rate - side_rate
        pos = spread(cy) > 0.0

        @pl.loop(0, tall // SUB)
        def _(part):
            for u in range(SUB):
                at = pl.ds(pl.multiple_of((part * SUB + u) * SUB, SUB), SUB)
                mask_now[at, :] = jnp.where(pos, mask_pos[at, :], mask_neg[at, :])

        zero = jnp.zeros((SUB, LANES), f32)

        def part(i, carry):
            held_rows = [list(pair) for pair in carry[0]]
            masks = list(carry[1])
            for u in range(SUB):
                at = pl.ds(pl.multiple_of((i * SUB + u) * SUB, SUB), SUB)
                value = wide[k, at, :]
                for stage in range(SIDE):
                    previous, current = held_rows[stage]
                    moved = (
                        keep * current
                        + down_rate * previous
                        + up_rate * value
                        + side_rate * pltpu.roll(current, 1, 0)
                    )
                    held_rows[stage] = [current, value]
                    value = moved * masks[stage]
                swept[at, :] = value
                masks = [mask_now[at, :]] + masks[: SIDE - 1]
            return tuple(tuple(pair) for pair in held_rows), tuple(masks)

        start = (tuple((zero, zero) for _ in range(SIDE)), (zero,) * SIDE)
        lax.fori_loop(0, tall // SUB, part, start)
        wanted = jnp.broadcast_to(cy > 0.0, (rows, LANES))
        columns = [
            swept[pl.ds(2 * SIDE * SUB + SIDE + q, rows, stride=SUB), :] for q in range(SIDE)
        ]
        for c in range(SIDE):
            back[k, c] = jnp.where(wanted, columns[c], columns[SIDE - 1 - c])
        home[k, y] = back[k, y]
        for d in (2, 1, 3):
            send_out(k, d).start()

    def finish(k):
        for d in (1, 2, 3):
            send_out(k, d).wait_recv()
        for m in range(SIDE):
            final[k, pl.ds(m, rows, stride=SIDE), :] = home[k, m]
        store(k).start()
        both = jnp.concatenate(split(final[k]), axis=1)
        term = jnp.dot(both, drift_kernel[k], preferred_element_type=f32)
        stokes[...] += term[:, :LANES] + term[:, LANES:]

    relax(0)
    pl.semaphore_wait(barrier, tiles)
    launch(0)
    for k in (1, 2):
        relax(k)
        launch(k)

    @pl.loop(0, 3)
    def _(i):
        for each in range(2):
            relax(3 + 2 * i + each)
            launch(3 + 2 * i + each)
        forward(i)

    prepare_masks()

    @pl.loop(0, chunks)
    def _(t):
        @pl.when(t + 3 < chunks)
        def _():
            forward(t + 3)

        @pl.when(t == 0)
        def _():
            prepare_kernel()

        @pl.when(t == 1)
        def _():
            prepare_slots()

        @pl.when(t == 2)
        def _():
            prepare_zeta()

        for side in range(2):
            send_halo(t, side).wait_recv()
        assemble(t)
        send_edge(t).start()

        @pl.when(t >= 2)
        def _():
            finish(t - 2)

        send_edge(t).wait_recv()
        sweep(t)

    @pl.loop(chunks - 2, chunks)
    def _(k):
        finish(k)

    both = jnp.concatenate(split(stokes[...]), axis=1)
    per = tiles // 4
    for part in range(4):
        span = per * slots
        term = jnp.dot(
            placer[part * span : (part + 1) * span, :], both, preferred_element_type=f32
        )
        posted[part * per : (part + 1) * per] = (term[:, :LANES] + term[:, LANES:]).reshape(
            per, slots, LANES
        )

    @pl.loop(1, tiles)
    def _(d):
        post(d).start()

    arrived[place] = posted[place]

    @pl.loop(0, chunks)
    def _(k):
        for d in (1, 2, 3):
            send_in(k, d).wait_send()
            send_out(k, d).wait_send()
        for side in range(2):
            send_halo(k, side).wait_send()
        send_edge(k).wait_send()
        store(k).wait()

    def all_of(ref, sem):
        some = ref.at[pl.ds(0, tiles - 1)]
        return pltpu.make_async_copy(some, some, sem)

    all_of(arrived, post_recv).wait()
    rows_in = arrived[...].reshape(tiles * slots, LANES)
    target = rows_in[:, drifts : drifts + 1]
    column = lax.broadcasted_iota(i32, (tiles * slots, cols), 1).astype(f32) + 1.0
    chosen = (target == column).astype(bf16)
    summed = lax.dot_general(
        jnp.concatenate(split(rows_in), axis=1),
        chosen,
        (((0,), (0,)), ((), ())),
        preferred_element_type=f32,
    )
    summed = summed[:LANES] + summed[LANES:]
    count = jnp.maximum(summed[drifts + 1 : drifts + 2], 1.0)
    east_drift = summed[:levels] / count
    north_drift = summed[levels:drifts] / count
    spin = coriolis[...]
    turn = spin + zeta[...]
    east, north = velocity[0], velocity[1]
    velocity_out[0] = east + 0.25 * (spin * north + turn * north_drift)
    velocity_out[1] = north - 0.25 * (spin * east + turn * east_drift)
    all_of(posted, post_send).wait()


def per_device(
    spectrum,
    interaction,
    comp_speed,
    sea_mask,
    stokes_kernel,
    tile_owner,
    ocean_column,
    neighbours,
    coriolis,
    velocity,
):
    held, comps = spectrum.shape[1:]
    chunks = comps // LANES
    rows = held // SIDE
    tall = rows + 2 * SIDE
    tiles = lax.axis_size("pts")
    slots = 16
    levels, cols = velocity.shape[2:]
    f32, bf16 = jnp.float32, jnp.bfloat16
    piece = pltpu.VMEM((chunks, SIDE, rows, LANES), f32)
    mask = pltpu.VMEM((tall * SUB, LANES), f32)
    vmem = pl.BlockSpec(memory_space=pltpu.VMEM)
    anywhere = pl.BlockSpec(memory_space=pl.ANY)
    dma = pltpu.SemaphoreType.DMA
    spectrum_next, velocity_next = pl.pallas_call(
        wave_kernel,
        out_shape=(
            jax.ShapeDtypeStruct((held, comps), f32),
            jax.ShapeDtypeStruct((2, levels, cols), f32),
        ),
        in_specs=[anywhere, anywhere] + [vmem] * 8,
        out_specs=(anywhere, vmem),
        scratch_shapes=[
            pltpu.VMEM((chunks, held, LANES), f32),
            pltpu.VMEM((chunks, comps, LANES), bf16),
            pltpu.VMEM((held, comps), bf16),
            piece,
            piece,
            piece,
            piece,
            pltpu.VMEM((chunks, tall * SUB, LANES), f32),
            mask,
            piece,
            piece,
            pltpu.VMEM((chunks, held, LANES), f32),
            mask,
            mask,
            mask,
            pltpu.VMEM((2 * rows, GC), f32),
            pltpu.VMEM((chunks, 2 * LANES, 2 * LANES), bf16),
            pltpu.VMEM((held, LANES), f32),
            pltpu.VMEM((tiles * slots, held), bf16),
            pltpu.VMEM((levels, cols), f32),
            pltpu.VMEM((tiles, slots, LANES), f32),
            pltpu.VMEM((tiles, slots, LANES), f32),
            dma((2, chunks)),
            dma((chunks,)),
            dma((chunks, 3)),
            dma((chunks, 3)),
            dma((chunks, 2)),
            dma((chunks, 2)),
            dma((chunks,)),
            dma((chunks,)),
            dma((chunks, 3)),
            dma((chunks, 3)),
            dma(()),
            dma(()),
        ],
        compiler_params=pltpu.CompilerParams(
            collective_id=0, has_side_effects=True, vmem_limit_bytes=56 << 20
        ),
        name="wave_step",
    )(
        spectrum[0],
        interaction,
        comp_speed,
        sea_mask,
        stokes_kernel,
        tile_owner[0],
        ocean_column,
        neighbours[0],
        coriolis,
        velocity[0],
    )
    return (spectrum_next[None], velocity_next[None])


def solution(mesh):
    placed = (
        P("grid", "pts", None),
        P(),
        P(),
        P(),
        P(),
        P("grid", "pts", None),
        P("grid", "pts"),
        P("grid", "pts", None),
        P("grid", "pts"),
        P("grid", None, None, "pts"),
    )
    return jax.shard_map(
        per_device,
        mesh=mesh,
        in_specs=placed,
        out_specs=(P("grid", "pts", None), P("grid", None, None, "pts")),
        check_vma=False,
    )
```

time: 143 us -> 133 us (0.930)
  Pallas kernels: 104 us -> 122 us
  waiting for transfers between devices: 12.4 us -> 0 us
  starting transfers between devices: 11.3 us -> 0 us
  matrix products: 4.16 us -> 0 us
  other arithmetic: 3.54 us -> 0 us
  local copies, waits for them, and re-layouts: 6.29 us -> 8.73 us
    pallas_call x1, Pallas kernels: 104 us -> 122 us  [per_device(): pl.pallas_call(wave_kernel, out_shape=(jax.ShapeDtypeStruct((held, comps)...]
    all_to_all x1 -> x0, waiting for transfers between devices: 12.4 us -> none  [per_device(): lax.all_to_all(buffer, 'pts', split_axis=0, concat_axis=0, tiled=True)]
    all_to_all x1 -> x0, starting transfers between devices: 11.3 us -> none  [per_device(): lax.all_to_all(buffer, 'pts', split_axis=0, concat_axis=0, tiled=True)]
    unnamed x10 -> x6, local copies, waits for them, and re-layouts: 2.55 us -> 7.2 us
    dot_general x6 -> x0, matrix products: 4.16 us -> none  [the longest x1 2.72 us: per_device(): jnp.dot(placer.T, payload, precision=lax.Precision.HIGHEST, preferred_ele...]
    reshape x3 -> x0, local copies, waits for them, and re-layouts: 2.73 us -> none  [the longest x1 1.86 us: per_device(): sea = sea_mask.reshape(-1, GC)]
    squeeze x0 -> x1, local copies, waits for them, and re-layouts: none -> 1.53 us  [per_device(): tile_owner[0]]
  transfers between devices with their start and end apart: 1 -> 0, of which waited for: 1 -> 0; matrix products, arithmetic and copies ran while one was open for 0% -> 0% of each run, Pallas kernels for 0% -> 0%
where the time goes in v2:
time: 133 us; the launch traced here: 132 us
  Pallas kernels  122 us (92%)
  local copies, waits for them, and re-layouts  8.73 us (7%)
    pallas_call x1, Pallas kernels, per_device(): pl.pallas_call(wave_kernel, out_shape=(jax.ShapeDtypeStruct((held, comps)...  122 us
    unnamed x6, local copies, waits for them, and re-layouts  7.2 us

profile of v2, /device:TPU:0, one launch (start us, length us, event | category | flops | bytes accessed | tf_op | source)
XLA Modules:
  0.0 131.6 jit_solution(10483916350824908437)
XLA Ops:
  0.6 1.5 %copy.14 = s32[1,256,4]{2,1,0:T(8,128)} copy(s32[1,256,4]{1,2,0:T(4,128)} %param.17) | data formatting | bytes 8192 | tf_op args[7]
  2.1 1.5 %copy.16.owner = s32[448,1]{1,0:T(8,128)} copy(s32[448,1]{0,1:T(1,128)} %bitcast.11) | data formatting | bytes 3584 | tf_op jit(solution)/shard_map/squeeze | solution.py:520
  3.6 2.0 %copy.15.kern = f32[1152,80]{1,0:T(8,128)} copy(f32[1152,80]{0,1:T(8,128)} %param.14) | data formatting | bytes 737280 | tf_op args[4]
  5.7 122.2 %wave_step.1 = (f32[448,1152]{1,0:T(8,128)}, f32[2,40,256]{2,1,0:T(8,128)}) custom-call(f32[448,1152]{1,0:T(8,128)} %bitcast.6, bf16[1152,1152]{1,0:T(8,128)(2,1)} %inter_hbm.1, f32[2,1152]{1,0:T(2,128)} %speed.1, s32[2,28672]{1,0:T(2,128)} %sea.1, f32[1152,80]{1,0:T(8,128)} %copy.15.kern, s32[448,1]{1,0:T(8,128)} %copy.16.owner, s32[1,448]{1,0:T(1,128)} %ocean.1, ...), custom_call_target="tpu_custom_call" | custom-call | tf_op jit(solution)/shard_map/wave_step/pallas_call | solution.py:466
  127.9 0.0 copy-start
  127.9 3.0 %copy.19 = f32[1,448,1152]{2,1,0:T(8,128)} copy(f32[1,448,1152]{2,1,0:T(8,128)} %bitcast.7) | data formatting | bytes 4128768
  131.0 0.0 copy-done
  131.0 0.6 copy.20
Async XLA Ops:
  127.9 3.1 %copy-start = (f32[2,40,256]{2,1,0:T(8,128)S(1)}, f32[2,40,256]{2,1,0:T(8,128)}, u32[]{:S(2)}) copy-start(f32[2,40,256]{2,1,0:T(8,128)} %get-tuple-element.5) | copy-start | bytes 245764

commit v3 on v2

--- a/solution.py
+++ b/solution.py
@@ -65,20 +65,32 @@
     rows = held // SIDE
     tall = rows + 2 * SIDE
     tiles, slots = arrived.shape[:2]
-    drifts = kern.shape[1]
+    drifts = kern.shape[0]
     levels = drifts // 2
     cols = coriolis.shape[1]
     grid = lax.axis_index("grid")
     place = lax.axis_index("pts")
     y = lax.rem(place, SIDE)
     base = place - y
-    block = 16 * y + place // SIDE
-    after = lax.rem(block + 1, 64)
-    before = lax.rem(block + 63, 64)
-    after_dev = SIDE * lax.rem(after, 16) + after // 16
-    before_dev = SIDE * lax.rem(before, 16) + before // 16
+    rings = tiles // SIDE
+    ring = place // SIDE
     peers = [base + lax.rem(y + d, SIDE) for d in (1, 2, 3)]
     lanes = lambda k: pl.ds(pl.multiple_of(k * LANES, LANES), LANES)
+
+    def turned(k, r):
+        return (r - (k + k // 3) + rings - 1) // rings
+
+    def group(k):
+        return lax.rem(y - turned(k, ring) + SIDE, SIDE)
+
+    def block(k):
+        return rings * group(k) + ring
+
+    def beside(k, step):
+        other = lax.rem(ring + step + rings, rings)
+        across = (ring + step + rings) // rings - 1
+        turn = across + turned(k, other) - turned(k, ring)
+        return SIDE * other + lax.rem(y + turn + 2 * SIDE, SIDE)
 
     def load_spec(k):
         return pltpu.make_async_copy(spec_hbm.at[:, lanes(k)], spec.at[k], load_sem.at[0, k])
@@ -113,7 +125,7 @@
 
     def send_in(k, d):
         return pltpu.make_async_remote_copy(
-            src_ref=sent.at[k, lax.rem(y + d, SIDE)],
+            src_ref=sent.at[k, lax.rem(group(k) + d, SIDE)],
             dst_ref=own.at[k, y],
             send_sem=in_send.at[k, d - 1],
             recv_sem=in_recv.at[k, d - 1],
@@ -127,7 +139,7 @@
             dst_ref=(left if side == 0 else right).at[k],
             send_sem=halo_send.at[k, side],
             recv_sem=halo_recv.at[k, side],
-            device_id={"pts": after_dev if side == 0 else before_dev},
+            device_id={"pts": beside(k, 1 if side == 0 else -1)},
             device_id_type=MESH,
         )
 
@@ -146,7 +158,7 @@
     def send_out(k, d):
         return pltpu.make_async_remote_copy(
             src_ref=back.at[k, lax.rem(y + d, SIDE)],
-            dst_ref=home.at[k, y],
+            dst_ref=home.at[k, group(k)],
             send_sem=out_send.at[k, d - 1],
             recv_sem=out_recv.at[k, d - 1],
             device_id={"pts": peers[d - 1]},
@@ -174,7 +186,7 @@
         for m in range(SIDE):
             local = spec[k, pl.ds(m, rows, stride=SIDE), :]
             sent[k, m] = local + 0.5 * local * grown[m * rows : (m + 1) * rows]
-        own[k, y] = sent[k, y]
+        own[k, y] = sent[k, group(k)]
 
     def launch(k):
         for d in (2, 1, 3):
@@ -201,15 +213,17 @@
             preferred_element_type=f32,
         ).astype(bf16)
         column = lax.broadcasted_iota(i32, (GC, LANES), 0)
-        for s in range(SUB):
-            first = (column == SIDE * block - SIDE + s).astype(bf16)
-            second = (column == SIDE * block + 7 - s).astype(bf16)
-            mask_pos[pl.ds(s, tall, stride=SUB), :] = jnp.dot(
-                picked, first, preferred_element_type=f32
-            )
-            mask_neg[pl.ds(s, tall, stride=SUB), :] = jnp.dot(
-                picked, second, preferred_element_type=f32
-            )
+        for turn in range(2):
+            start = SIDE * (rings * lax.rem(y - turn + SIDE, SIDE) + ring)
+            for s in range(SUB):
+                first = (column == start - SIDE + s).astype(bf16)
+                second = (column == start + 7 - s).astype(bf16)
+                mask_pos[turn, pl.ds(s, tall, stride=SUB), :] = jnp.dot(
+                    picked, first, preferred_element_type=f32
+                )
+                mask_neg[turn, pl.ds(s, tall, stride=SUB), :] = jnp.dot(
+                    picked, second, preferred_element_type=f32
+                )
 
     def split(value):
         high = value.astype(bf16)
@@ -218,17 +232,18 @@
     def prepare_kernel():
         drift_kernel[...] = jnp.zeros_like(drift_kernel)
         for k in range(chunks):
-            high, low = split(kern[k * LANES : (k + 1) * LANES, :])
-            drift_kernel[k, 0:LANES, 0:drifts] = high
-            drift_kernel[k, 0:LANES, LANES : LANES + drifts] = low
-            drift_kernel[k, LANES : 2 * LANES, 0:drifts] = high
+            high, low = split(kern[:, k * LANES : (k + 1) * LANES])
+            drift_kernel[k, 0:drifts, 0:LANES] = high
+            drift_kernel[k, 0:drifts, LANES : 2 * LANES] = high
+            drift_kernel[k, LANES : LANES + drifts, 0:LANES] = low
 
     def prepare_slots():
         down = lax.broadcasted_iota(i32, (held, held), 0)
         across = lax.broadcasted_iota(i32, (held, held), 1)
-        owners = jnp.broadcast_to(owner[...].astype(f32), (held, held))
-        owner_row = jnp.sum(jnp.where(down == across, owners, 0.0), axis=0, keepdims=True)
-        earlier = (owners == owner_row) & (down < across)
+        owner_row = owner[...].astype(f32)
+        owners = jnp.broadcast_to(owner_row, (held, held))
+        owner_column = jnp.sum(jnp.where(down == across, owners, 0.0), axis=1, keepdims=True)
+        earlier = (owners == owner_column) & (down < across)
         rank = jnp.sum(jnp.where(earlier, 1.0, 0.0), axis=0, keepdims=True)
         slot = owner_row * slots + rank
         for part in range(tiles * slots // LANES):
@@ -240,11 +255,11 @@
         stokes[...] = jnp.where(lane == drifts, target, jnp.where(lane == drifts + 1, 1.0, 0.0))
 
     def prepare_zeta():
-        column = lax.broadcasted_iota(i32, (cols, cols), 1)
+        column = lax.broadcasted_iota(i32, (cols, cols), 0)
 
         def apart(first, second):
-            one = (near[:, first : first + 1] == column).astype(f32)
-            two = (near[:, second : second + 1] == column).astype(f32)
+            one = (near[first : first + 1, :] == column).astype(f32)
+            two = (near[second : second + 1, :] == column).astype(f32)
             return (one - two).astype(bf16)
 
         def taken(flow, picker):
@@ -252,17 +267,15 @@
             rest = (flow - high.astype(f32) - low.astype(f32)).astype(bf16)
             total = jnp.zeros(flow.shape, f32)
             for each in (high, low, rest):
-                total += lax.dot_general(
-                    each, picker, (((1,), (1,)), ((), ())), preferred_element_type=f32
-                )
+                total += jnp.dot(each, picker, preferred_element_type=f32)
             return total
 
         zeta[...] = taken(velocity[1], apart(0, 1)) - taken(velocity[0], apart(2, 3))
 
     def assemble(k):
         pos = jnp.broadcast_to(speed[1:2, lanes(k)] > 0.0, (rows, LANES))
-        from_left = block > 0
-        from_right = block < 63
+        from_left = block(k) > 0
+        from_right = block(k) < tiles - 1
         for s in range(SIDE):
             lower = jnp.where(from_left, left[k, s], 0.0)
             upper = jnp.where(from_right, right[k, SIDE - 1 - s], 0.0)
@@ -283,12 +296,13 @@
         side_rate = spread(jnp.abs(cy))
         keep = 1.0 - down_rate - up_rate - side_rate
         pos = spread(cy) > 0.0
+        turn = turned(k, ring)
 
         @pl.loop(0, tall // SUB)
         def _(part):
             for u in range(SUB):
                 at = pl.ds(pl.multiple_of((part * SUB + u) * SUB, SUB), SUB)
-                mask_now[at, :] = jnp.where(pos, mask_pos[at, :], mask_neg[at, :])
+                mask_now[at, :] = jnp.where(pos, mask_pos[turn, at, :], mask_neg[turn, at, :])
 
         zero = jnp.zeros((SUB, LANES), f32)
 
@@ -320,7 +334,7 @@
         ]
         for c in range(SIDE):
             back[k, c] = jnp.where(wanted, columns[c], columns[SIDE - 1 - c])
-        home[k, y] = back[k, y]
+        home[k, group(k)] = back[k, y]
         for d in (2, 1, 3):
             send_out(k, d).start()
 
@@ -331,7 +345,9 @@
             final[k, pl.ds(m, rows, stride=SIDE), :] = home[k, m]
         store(k).start()
         both = jnp.concatenate(split(final[k]), axis=1)
-        term = jnp.dot(both, drift_kernel[k], preferred_element_type=f32)
+        term = lax.dot_general(
+            both, drift_kernel[k], (((1,), (1,)), ((), ())), preferred_element_type=f32
+        )
         stokes[...] += term[:, :LANES] + term[:, LANES:]
 
     relax(0)
@@ -484,8 +500,8 @@
             piece,
             piece,
             pltpu.VMEM((chunks, held, LANES), f32),
-            mask,
-            mask,
+            pltpu.VMEM((2, tall * SUB, LANES), f32),
+            pltpu.VMEM((2, tall * SUB, LANES), f32),
             mask,
             pltpu.VMEM((2 * rows, GC), f32),
             pltpu.VMEM((chunks, 2 * LANES, 2 * LANES), bf16),
@@ -516,10 +532,10 @@
         interaction,
         comp_speed,
         sea_mask,
-        stokes_kernel,
-        tile_owner[0],
+        stokes_kernel.T,
+        tile_owner.reshape(1, held),
         ocean_column,
-        neighbours[0],
+        neighbours[0].T,
         coriolis,
         velocity[0],
     )

time: 133 us -> 86.3 us (0.65)
  Pallas kernels: 122 us -> 81.4 us
  local copies, waits for them, and re-layouts: 8.73 us -> 3.69 us
    pallas_call x1, Pallas kernels: 122 us -> 81.4 us  [per_device(): pl.pallas_call(wave_kernel, out_shape=(jax.ShapeDtypeStruct((held, comps)...]
    unnamed x6 -> x4, local copies, waits for them, and re-layouts: 7.2 us -> 3.69 us
    squeeze x1 -> x0, local copies, waits for them, and re-layouts: 1.53 us -> none  [per_device(): tile_owner[0]]
where the time goes in v3:
time: 86.3 us; the launch traced here: 85.7 us
  Pallas kernels  81.4 us (94%)
  local copies, waits for them, and re-layouts  3.69 us (4%)
    pallas_call x1, Pallas kernels, per_device(): pl.pallas_call(wave_kernel, out_shape=(jax.ShapeDtypeStruct((held, comps)...  81.4 us
    unnamed x4, local copies, waits for them, and re-layouts  3.69 us

profile of v3, /device:TPU:0, one launch (start us, length us, event | category | flops | bytes accessed | tf_op | source)
XLA Modules:
  0.0 85.7 jit_solution(13667744806373747022)
XLA Ops:
  0.6 81.4 %wave_step.1 = (f32[448,1152]{1,0:T(8,128)}, f32[2,40,256]{2,1,0:T(8,128)}) custom-call(f32[448,1152]{1,0:T(8,128)} %bitcast.9, bf16[1152,1152]{1,0:T(8,128)(2,1)} %inter_hbm.1, f32[2,1152]{1,0:T(2,128)} %speed.1, s32[2,28672]{1,0:T(2,128)} %sea.1, f32[80,1152]{1,0:T(8,128)} %bitcast.11, s32[1,448]{1,0:T(1,128)} %bitcast.15, s32[1,448]{1,0:T(1,128)} %ocean.1, ...), custom_call_target="tpu_custom_call" | custom-call | tf_op jit(solution)/shard_map/wave_step/pallas_call | solution.py:482
  82.0 0.0 copy-start
  82.0 3.0 %copy.14 = f32[1,448,1152]{2,1,0:T(8,128)} copy(f32[1,448,1152]{2,1,0:T(8,128)} %bitcast.10) | data formatting | bytes 4128768
  85.1 0.0 copy-done
  85.1 0.6 copy.15
Async XLA Ops:
  82.0 3.1 %copy-start = (f32[2,40,256]{2,1,0:T(8,128)S(1)}, f32[2,40,256]{2,1,0:T(8,128)}, u32[]{:S(2)}) copy-start(f32[2,40,256]{2,1,0:T(8,128)} %get-tuple-element.5) | copy-start | bytes 245764

commit v4 on v3

--- a/solution.py
+++ b/solution.py
@@ -15,16 +15,23 @@
 def wave_kernel(
     spec_hbm,
     inter_hbm,
-    speed,
+    sea_hbm,
+    kern_hbm,
+    velocity_hbm,
+    speed_hbm,
+    owner_hbm,
+    ocean_hbm,
+    near_hbm,
+    out_hbm,
+    arrived_out,
+    zeta,
     sea,
     kern,
+    velocity,
+    speed,
     owner,
     ocean,
     near,
-    coriolis,
-    velocity,
-    out_hbm,
-    velocity_out,
     spec,
     inter,
     half,
@@ -44,10 +51,10 @@
     drift_kernel,
     stokes,
     placer,
-    zeta,
     posted,
     arrived,
     load_sem,
+    side_sem,
     store_sem,
     in_send,
     in_recv,
@@ -59,6 +66,8 @@
     out_recv,
     post_send,
     post_recv,
+    first_send,
+    first_recv,
 ):
     f32, bf16, i32 = jnp.float32, jnp.bfloat16, jnp.int32
     chunks, held = spec.shape[:2]
@@ -66,8 +75,7 @@
     tall = rows + 2 * SIDE
     tiles, slots = arrived.shape[:2]
     drifts = kern.shape[0]
-    levels = drifts // 2
-    cols = coriolis.shape[1]
+    cols = near.shape[1]
     grid = lax.axis_index("grid")
     place = lax.axis_index("pts")
     y = lax.rem(place, SIDE)
@@ -116,6 +124,23 @@
     def _(k):
         load_inter(k).start()
 
+    side_loads = [
+        pltpu.make_async_copy(source, target, side_sem.at[i])
+        for i, (source, target) in enumerate(
+            [
+                (sea_hbm, sea),
+                (kern_hbm, kern),
+                (velocity_hbm, velocity),
+                (speed_hbm, speed),
+                (owner_hbm, owner),
+                (ocean_hbm, ocean),
+                (near_hbm, near),
+            ]
+        )
+    ]
+    for each in side_loads:
+        each.start()
+
     for k in range(chunks):
         load_spec(k).wait()
         for m in range(SIDE):
@@ -140,6 +165,16 @@
             send_sem=halo_send.at[k, side],
             recv_sem=halo_recv.at[k, side],
             device_id={"pts": beside(k, 1 if side == 0 else -1)},
+            device_id_type=MESH,
+        )
+
+    def send_first(c, side):
+        return pltpu.make_async_remote_copy(
+            src_ref=own.at[0, c],
+            dst_ref=(left if side == 0 else right).at[0, c],
+            send_sem=first_send.at[c, side],
+            recv_sem=first_recv.at[c, side],
+            device_id={"pts": beside(0, 1 if side == 0 else -1)},
             device_id_type=MESH,
         )
 
@@ -165,8 +200,7 @@
             device_id_type=MESH,
         )
 
-    def post(d):
-        peer = lax.rem(place + d, tiles)
+    def post(peer):
         return pltpu.make_async_remote_copy(
             src_ref=posted.at[peer],
             dst_ref=arrived.at[place],
@@ -225,10 +259,6 @@
                     picked, second, preferred_element_type=f32
                 )
 
-    def split(value):
-        high = value.astype(bf16)
-        return high, (value - high.astype(f32)).astype(bf16)
-
     def prepare_kernel():
         drift_kernel[...] = jnp.zeros_like(drift_kernel)
         for k in range(chunks):
@@ -353,17 +383,25 @@
     relax(0)
     pl.semaphore_wait(barrier, tiles)
     launch(0)
+    for side in range(2):
+        send_first(y, side).start()
     for k in (1, 2):
         relax(k)
         launch(k)
-
-    @pl.loop(0, 3)
+    for d in (1, 3, 2):
+        send_in(0, d).wait_recv()
+        for side in range(2):
+            send_first(lax.rem(y - d + SIDE, SIDE), side).start()
+
+    @pl.loop(1, 3)
     def _(i):
-        for each in range(2):
-            relax(3 + 2 * i + each)
-            launch(3 + 2 * i + each)
+        for each in range(3):
+            relax(3 * i + each)
+            launch(3 * i + each)
         forward(i)
 
+    for each in side_loads:
+        each.wait()
     prepare_masks()
 
     @pl.loop(0, chunks)
@@ -384,8 +422,17 @@
         def _():
             prepare_zeta()
 
-        for side in range(2):
-            send_halo(t, side).wait_recv()
+        @pl.when(t == 0)
+        def _():
+            for side in range(2):
+                for c in range(SIDE):
+                    send_first(c, side).wait_recv()
+
+        @pl.when(t > 0)
+        def _():
+            for side in range(2):
+                send_halo(t, side).wait_recv()
+
         assemble(t)
         send_edge(t).start()
 
@@ -401,19 +448,22 @@
         finish(k)
 
     both = jnp.concatenate(split(stokes[...]), axis=1)
-    per = tiles // 4
-    for part in range(4):
-        span = per * slots
+    parts = 4
+    per = tiles // parts
+    for step in range(parts):
+        part = lax.rem(place // per + step, parts)
         term = jnp.dot(
-            placer[part * span : (part + 1) * span, :], both, preferred_element_type=f32
-        )
-        posted[part * per : (part + 1) * per] = (term[:, :LANES] + term[:, LANES:]).reshape(
+            placer[pl.ds(pl.multiple_of(part * per * slots, LANES), per * slots), :],
+            both,
+            preferred_element_type=f32,
+        )
+        posted[pl.ds(part * per, per)] = (term[:, :LANES] + term[:, LANES:]).reshape(
             per, slots, LANES
         )
 
-    @pl.loop(1, tiles)
-    def _(d):
-        post(d).start()
+        @pl.loop(1 if step == 0 else 0, per)
+        def _(d):
+            post(part * per + lax.rem(place + d, per)).start()
 
     arrived[place] = posted[place]
 
@@ -422,20 +472,49 @@
         for d in (1, 2, 3):
             send_in(k, d).wait_send()
             send_out(k, d).wait_send()
+        send_edge(k).wait_send()
+        store(k).wait()
+
+    @pl.loop(1, chunks)
+    def _(k):
         for side in range(2):
             send_halo(k, side).wait_send()
-        send_edge(k).wait_send()
-        store(k).wait()
+
+    for side in range(2):
+        for c in range(SIDE):
+            send_first(c, side).wait_send()
 
     def all_of(ref, sem):
         some = ref.at[pl.ds(0, tiles - 1)]
         return pltpu.make_async_copy(some, some, sem)
 
     all_of(arrived, post_recv).wait()
-    rows_in = arrived[...].reshape(tiles * slots, LANES)
+    arrived_out[...] = arrived[...].reshape(tiles * slots, LANES)
+    all_of(posted, post_send).wait()
+
+
+def split(value):
+    high = value.astype(jnp.bfloat16)
+    return high, (value - high.astype(jnp.float32)).astype(jnp.bfloat16)
+
+
+def ocean_kernel(profiles, waves, zeta, coriolis, velocity, out_hbm, velocity_out, give_sem):
+    f32 = jnp.float32
+    pieces = give_sem.shape[0]
+    span = waves.shape[0] // pieces
+
+    def give(i):
+        at = pl.ds(i * span, span)
+        return pltpu.make_async_copy(waves.at[at], out_hbm.at[at], give_sem.at[i])
+
+    for i in range(pieces):
+        give(i).start()
+    levels, cols = zeta.shape
+    drifts = 2 * levels
+    rows_in = profiles[...]
     target = rows_in[:, drifts : drifts + 1]
-    column = lax.broadcasted_iota(i32, (tiles * slots, cols), 1).astype(f32) + 1.0
-    chosen = (target == column).astype(bf16)
+    column = lax.broadcasted_iota(jnp.int32, (rows_in.shape[0], cols), 1).astype(f32) + 1.0
+    chosen = (target == column).astype(jnp.bfloat16)
     summed = lax.dot_general(
         jnp.concatenate(split(rows_in), axis=1),
         chosen,
@@ -451,7 +530,8 @@
     east, north = velocity[0], velocity[1]
     velocity_out[0] = east + 0.25 * (spin * north + turn * north_drift)
     velocity_out[1] = north - 0.25 * (spin * east + turn * east_drift)
-    all_of(posted, post_send).wait()
+    for i in range(pieces):
+        give(i).wait()
 
 
 def per_device(
@@ -478,16 +558,25 @@
     mask = pltpu.VMEM((tall * SUB, LANES), f32)
     vmem = pl.BlockSpec(memory_space=pltpu.VMEM)
     anywhere = pl.BlockSpec(memory_space=pl.ANY)
+    hbm = pl.BlockSpec(memory_space=pltpu.HBM)
     dma = pltpu.SemaphoreType.DMA
-    spectrum_next, velocity_next = pl.pallas_call(
+    waves, profiles, zeta = pl.pallas_call(
         wave_kernel,
         out_shape=(
             jax.ShapeDtypeStruct((held, comps), f32),
-            jax.ShapeDtypeStruct((2, levels, cols), f32),
+            jax.ShapeDtypeStruct((tiles * slots, LANES), f32),
+            jax.ShapeDtypeStruct((levels, cols), f32),
         ),
-        in_specs=[anywhere, anywhere] + [vmem] * 8,
-        out_specs=(anywhere, vmem),
+        in_specs=[hbm] * 9,
+        out_specs=(anywhere, vmem, vmem),
         scratch_shapes=[
+            pltpu.VMEM(sea_mask.shape, sea_mask.dtype),
+            pltpu.VMEM(stokes_kernel.shape[::-1], f32),
+            pltpu.VMEM((2, levels, cols), f32),
+            pltpu.VMEM(comp_speed.shape, f32),
+            pltpu.VMEM((1, held), jnp.int32),
+            pltpu.VMEM((1, held), jnp.int32),
+            pltpu.VMEM((neighbours.shape[2], cols), jnp.int32),
             pltpu.VMEM((chunks, held, LANES), f32),
             pltpu.VMEM((chunks, comps, LANES), bf16),
             pltpu.VMEM((held, comps), bf16),
@@ -507,10 +596,10 @@
             pltpu.VMEM((chunks, 2 * LANES, 2 * LANES), bf16),
             pltpu.VMEM((held, LANES), f32),
             pltpu.VMEM((tiles * slots, held), bf16),
-            pltpu.VMEM((levels, cols), f32),
             pltpu.VMEM((tiles, slots, LANES), f32),
             pltpu.VMEM((tiles, slots, LANES), f32),
             dma((2, chunks)),
+            dma((7,)),
             dma((chunks,)),
             dma((chunks, 3)),
             dma((chunks, 3)),
@@ -522,23 +611,41 @@
             dma((chunks, 3)),
             dma(()),
             dma(()),
+            dma((SIDE, 2)),
+            dma((SIDE, 2)),
         ],
         compiler_params=pltpu.CompilerParams(
-            collective_id=0, has_side_effects=True, vmem_limit_bytes=56 << 20
+            collective_id=0, has_side_effects=True, vmem_limit_bytes=36 << 20
         ),
         name="wave_step",
     )(
-        spectrum[0],
-        interaction,
-        comp_speed,
-        sea_mask,
-        stokes_kernel.T,
-        tile_owner.reshape(1, held),
-        ocean_column,
-        neighbours[0].T,
-        coriolis,
-        velocity[0],
+        *(
+            pltpu.with_memory_space_constraint(each, pltpu.HBM)
+            for each in (
+                spectrum[0],
+                interaction,
+                sea_mask,
+                stokes_kernel.T,
+                velocity[0],
+                comp_speed,
+                tile_owner.reshape(1, held),
+                ocean_column,
+                neighbours[0].T,
+            )
+        )
     )
+    spectrum_next, velocity_next = pl.pallas_call(
+        ocean_kernel,
+        out_shape=(
+            jax.ShapeDtypeStruct((held, comps), f32),
+            jax.ShapeDtypeStruct((2, levels, cols), f32),
+        ),
+        in_specs=[vmem] * 5,
+        out_specs=(hbm, vmem),
+        scratch_shapes=[dma((SIDE,))],
+        compiler_params=pltpu.CompilerParams(vmem_limit_bytes=8 << 20),
+        name="ocean_step",
+    )(profiles, waves, zeta, coriolis, velocity[0])
     return (spectrum_next[None], velocity_next[None])
 
 

time: 86.3 us -> 81.8 us (0.948)
  local copies, waits for them, and re-layouts: 3.69 us -> 0.01 us
    unnamed x4, local copies, waits for them, and re-layouts: 3.69 us -> 0.01 us
    pallas_call x1, Pallas kernels: 81.4 us -> 78.7 us  [per_device(): pl.pallas_call(wave_kernel, out_shape=(jax.ShapeDtypeStruct((held, comps)...]
    pallas_call x0 -> x1, Pallas kernels: none -> 1.98 us  [per_device(): pl.pallas_call(ocean_kernel, out_shape=(jax.ShapeDtypeStruct((held, comps...]
where the time goes in v4:
time: 81.8 us; the launch traced here: 81.4 us
  Pallas kernels  80.7 us (99%)
    pallas_call x1, Pallas kernels, per_device(): pl.pallas_call(wave_kernel, out_shape=(jax.ShapeDtypeStruct((held, comps)...  78.7 us
    pallas_call x1, Pallas kernels, per_device(): pl.pallas_call(ocean_kernel, out_shape=(jax.ShapeDtypeStruct((held, comps...  1.98 us

profile of v4, /device:TPU:0, one launch (start us, length us, event | category | flops | bytes accessed | tf_op | source)
XLA Modules:
  0.0 81.4 jit_solution(4257897983580616272)
XLA Ops:
  0.6 0.0 copy-start
  0.6 0.0 copy-start.1
  0.7 78.7 %wave_step.1 = (f32[448,1152]{1,0:T(8,128)S(1)}, f32[1024,128]{1,0:T(8,128)S(1)}, f32[40,256]{1,0:T(8,128)S(1)}) custom-call(f32[448,1152]{1,0:T(8,128)} %bitcast.11, bf16[1152,1152]{1,0:T(8,128)(2,1)} %inter_hbm.1, s32[2,28672]{1,0:T(2,128)} %sea_hbm.1, f32[80,1152]{1,0:T(8,128)} %bitcast.12, f32[2,40,256]{2,1,0:T(8,128)} %bitcast.9, f32[2,1152]{1,0:T(2,128)} %speed_hbm.1, ...), custom_call_target="tpu_custom_call" | custom-call | tf_op jit(solution)/shard_map/wave_step/pallas_call | solution.py:563
  79.4 0.0 copy-done
  79.4 0.0 copy-done.1
  79.4 2.0 %ocean_step.1 = (f32[448,1152]{1,0:T(8,128)}, f32[2,40,256]{2,1,0:T(8,128)}) custom-call(f32[1024,128]{1,0:T(8,128)S(1)} %get-tuple-element.7.profiles, f32[448,1152]{1,0:T(8,128)S(1)} %get-tuple-element.8.waves, f32[40,256]{1,0:T(8,128)S(1)} %get-tuple-element.9.zeta, f32[1,256]{1,0:T(1,128)S(1)} %copy-done.1, f32[2,40,256]{2,1,0:T(8,128)S(1)} %bitcast.10), custom_call_target="tpu_custom_call" | custom-call | tf_op jit(solution)/shard_map/ocean_step/pallas_call | solution.py:637
Async XLA Ops:
  0.6 78.8 %copy-start = (f32[1,2,40,256]{3,2,1,0:T(8,128)S(1)}, f32[1,2,40,256]{3,2,1,0:T(8,128)}, u32[]{:S(2)}) copy-start(f32[1,2,40,256]{3,2,1,0:T(8,128)} %param.19) | copy-start | bytes 245764
  0.6 78.8 %copy-start.1 = (f32[1,256]{1,0:T(1,128)S(1)}, f32[1,256]{1,0:T(1,128)}, u32[]{:S(2)}) copy-start(f32[1,256]{1,0:T(1,128)} %coriolis.1) | copy-start | bytes 3076

commit v5 on v4

--- a/solution.py
+++ b/solution.py
@@ -73,8 +73,11 @@
     chunks, held = spec.shape[:2]
     rows = held // SIDE
     tall = rows + 2 * SIDE
-    tiles, slots = arrived.shape[:2]
+    tiles = arrived.shape[0]
     drifts = kern.shape[0]
+    slots = arrived_out.shape[0] // tiles
+    parts = 4
+    per = tiles // parts
     cols = near.shape[1]
     grid = lax.axis_index("grid")
     place = lax.axis_index("pts")
@@ -168,13 +171,15 @@
             device_id_type=MESH,
         )
 
-    def send_first(c, side):
+    early = first_send.shape[0]
+
+    def send_first(k, c, side):
         return pltpu.make_async_remote_copy(
-            src_ref=own.at[0, c],
-            dst_ref=(left if side == 0 else right).at[0, c],
-            send_sem=first_send.at[c, side],
-            recv_sem=first_recv.at[c, side],
-            device_id={"pts": beside(0, 1 if side == 0 else -1)},
+            src_ref=own.at[k, c],
+            dst_ref=(left if side == 0 else right).at[k, c],
+            send_sem=first_send.at[k, c, side],
+            recv_sem=first_recv.at[k, c, side],
+            device_id={"pts": beside(k, 1 if side == 0 else -1)},
             device_id_type=MESH,
         )
 
@@ -275,14 +280,15 @@
         owner_column = jnp.sum(jnp.where(down == across, owners, 0.0), axis=1, keepdims=True)
         earlier = (owners == owner_column) & (down < across)
         rank = jnp.sum(jnp.where(earlier, 1.0, 0.0), axis=0, keepdims=True)
-        slot = owner_row * slots + rank
+        quarter = jnp.floor(owner_row / per)
+        slot = (quarter * slots + rank) * per + (owner_row - quarter * per)
         for part in range(tiles * slots // LANES):
             at = lax.broadcasted_iota(i32, (LANES, held), 0) + part * LANES
             placer[part * LANES : (part + 1) * LANES, :] = (at.astype(f32) == slot).astype(bf16)
         wanted = jnp.broadcast_to(ocean[...].astype(f32) + 1.0, (held, held))
         target = jnp.sum(jnp.where(down == across, wanted, 0.0), axis=1, keepdims=True)
         lane = lax.broadcasted_iota(i32, (held, LANES), 1)
-        stokes[...] = jnp.where(lane == drifts, target, jnp.where(lane == drifts + 1, 1.0, 0.0))
+        stokes[...] = jnp.where(lane == drifts, target, 0.0)
 
     def prepare_zeta():
         column = lax.broadcasted_iota(i32, (cols, cols), 0)
@@ -382,23 +388,24 @@
 
     relax(0)
     pl.semaphore_wait(barrier, tiles)
-    launch(0)
-    for side in range(2):
-        send_first(y, side).start()
-    for k in (1, 2):
+    for k in range(early):
+        if k > 0:
+            relax(k)
+        launch(k)
+        for side in range(2):
+            send_first(k, y, side).start()
+    ahead = 6
+    for k in range(early, ahead - early + 1):
         relax(k)
         launch(k)
-    for d in (1, 3, 2):
-        send_in(0, d).wait_recv()
-        for side in range(2):
-            send_first(lax.rem(y - d + SIDE, SIDE), side).start()
-
-    @pl.loop(1, 3)
-    def _(i):
-        for each in range(3):
-            relax(3 * i + each)
-            launch(3 * i + each)
-        forward(i)
+    for k in range(early):
+        for d in (1, 3, 2):
+            send_in(k, d).wait_recv()
+            for side in range(2):
+                send_first(k, lax.rem(y - d + SIDE, SIDE), side).start()
+        if ahead - early + 1 + k < ahead:
+            relax(ahead - early + 1 + k)
+            launch(ahead - early + 1 + k)
 
     for each in side_loads:
         each.wait()
@@ -406,6 +413,11 @@
 
     @pl.loop(0, chunks)
     def _(t):
+        @pl.when(t + 3 + 3 < chunks)
+        def _():
+            relax(t + 3 + 3)
+            launch(t + 3 + 3)
+
         @pl.when(t + 3 < chunks)
         def _():
             forward(t + 3)
@@ -422,13 +434,13 @@
         def _():
             prepare_zeta()
 
-        @pl.when(t == 0)
+        @pl.when(t < early)
         def _():
             for side in range(2):
                 for c in range(SIDE):
-                    send_first(c, side).wait_recv()
-
-        @pl.when(t > 0)
+                    send_first(t, c, side).wait_recv()
+
+        @pl.when(t >= early)
         def _():
             for side in range(2):
                 send_halo(t, side).wait_recv()
@@ -447,19 +459,28 @@
     def _(k):
         finish(k)
 
+    starts = [divmod(i * (drifts + 1), LANES) for i in range(slots)]
     both = jnp.concatenate(split(stokes[...]), axis=1)
-    parts = 4
-    per = tiles // parts
+    lane = lax.broadcasted_iota(jnp.int32, (per, LANES), 1)
     for step in range(parts):
         part = lax.rem(place // per + step, parts)
         term = jnp.dot(
-            placer[pl.ds(pl.multiple_of(part * per * slots, LANES), per * slots), :],
+            placer[pl.ds(pl.multiple_of(part * per * slots, 2 * SUB), per * slots), :],
             both,
             preferred_element_type=f32,
         )
-        posted[pl.ds(part * per, per)] = (term[:, :LANES] + term[:, LANES:]).reshape(
-            per, slots, LANES
-        )
+        packed = [jnp.zeros((per, LANES), f32) for _ in range(arrived.shape[1])]
+        for i, (row, at) in enumerate(starts):
+            mine = term[i * per : (i + 1) * per]
+            mine = mine[:, :LANES] + mine[:, LANES:]
+            if at:
+                mine = pltpu.roll(mine, at, 1)
+            end = at + drifts + 1
+            packed[row] = jnp.where((lane >= at) & (lane < end), mine, packed[row])
+            if end > LANES:
+                packed[row + 1] = jnp.where(lane < end - LANES, mine, packed[row + 1])
+        for row, values in enumerate(packed):
+            posted[pl.ds(part * per, per), row, :] = values
 
         @pl.loop(1 if step == 0 else 0, per)
         def _(d):
@@ -475,21 +496,30 @@
         send_edge(k).wait_send()
         store(k).wait()
 
-    @pl.loop(1, chunks)
+    @pl.loop(early, chunks)
     def _(k):
         for side in range(2):
             send_halo(k, side).wait_send()
 
-    for side in range(2):
-        for c in range(SIDE):
-            send_first(c, side).wait_send()
+    @pl.loop(0, early)
+    def _(k):
+        for side in range(2):
+            for c in range(SIDE):
+                send_first(k, c, side).wait_send()
 
     def all_of(ref, sem):
         some = ref.at[pl.ds(0, tiles - 1)]
         return pltpu.make_async_copy(some, some, sem)
 
     all_of(arrived, post_recv).wait()
-    arrived_out[...] = arrived[...].reshape(tiles * slots, LANES)
+    lane = lax.broadcasted_iota(jnp.int32, (tiles, LANES), 1)
+    for i, (row, at) in enumerate(starts):
+        taken = arrived[:, row, :]
+        if at + drifts + 1 > LANES:
+            taken = jnp.where(lane >= at, taken, arrived[:, row + 1, :])
+        if at:
+            taken = pltpu.roll(taken, LANES - at, 1)
+        arrived_out[i * tiles : (i + 1) * tiles, :] = jnp.where(lane == drifts + 1, 1.0, taken)
     all_of(posted, post_send).wait()
 
 
@@ -551,8 +581,9 @@
     rows = held // SIDE
     tall = rows + 2 * SIDE
     tiles = lax.axis_size("pts")
-    slots = 16
+    slots = 2 * held // tiles
     levels, cols = velocity.shape[2:]
+    packed = -(-slots * (2 * levels + 1) // LANES)
     f32, bf16 = jnp.float32, jnp.bfloat16
     piece = pltpu.VMEM((chunks, SIDE, rows, LANES), f32)
     mask = pltpu.VMEM((tall * SUB, LANES), f32)
@@ -596,8 +627,8 @@
             pltpu.VMEM((chunks, 2 * LANES, 2 * LANES), bf16),
             pltpu.VMEM((held, LANES), f32),
             pltpu.VMEM((tiles * slots, held), bf16),
-            pltpu.VMEM((tiles, slots, LANES), f32),
-            pltpu.VMEM((tiles, slots, LANES), f32),
+            pltpu.VMEM((tiles, packed, LANES), f32),
+            pltpu.VMEM((tiles, packed, LANES), f32),
             dma((2, chunks)),
             dma((7,)),
             dma((chunks,)),
@@ -611,8 +642,8 @@
             dma((chunks, 3)),
             dma(()),
             dma(()),
-            dma((SIDE, 2)),
-            dma((SIDE, 2)),
+            dma((3, SIDE, 2)),
+            dma((3, SIDE, 2)),
         ],
         compiler_params=pltpu.CompilerParams(
             collective_id=0, has_side_effects=True, vmem_limit_bytes=36 << 20

time: 81.8 us -> 78.6 us (0.961)
  Pallas kernels: 80.7 us -> 77.5 us
    pallas_call x1, Pallas kernels: 78.7 us -> 75.5 us  [per_device(): pl.pallas_call(wave_kernel, out_shape=(jax.ShapeDtypeStruct((held, comps)...]
where the time goes in v5:
time: 78.6 us; the launch traced here: 78.2 us
  Pallas kernels  77.5 us (99%)
    pallas_call x1, Pallas kernels, per_device(): pl.pallas_call(wave_kernel, out_shape=(jax.ShapeDtypeStruct((held, comps)...  75.5 us
    pallas_call x1, Pallas kernels, per_device(): pl.pallas_call(ocean_kernel, out_shape=(jax.ShapeDtypeStruct((held, comps...  1.98 us

profile of v5, /device:TPU:0, one launch (start us, length us, event | category | flops | bytes accessed | tf_op | source)
XLA Modules:
  0.0 78.2 jit_solution(9902459201724116680)
XLA Ops:
  0.6 0.0 copy-start
  0.6 0.0 copy-start.1
  0.7 75.5 %wave_step.1 = (f32[448,1152]{1,0:T(8,128)S(1)}, f32[896,128]{1,0:T(8,128)S(1)}, f32[40,256]{1,0:T(8,128)S(1)}) custom-call(f32[448,1152]{1,0:T(8,128)} %bitcast.11, bf16[1152,1152]{1,0:T(8,128)(2,1)} %inter_hbm.1, s32[2,28672]{1,0:T(2,128)} %sea_hbm.1, f32[80,1152]{1,0:T(8,128)} %bitcast.12, f32[2,40,256]{2,1,0:T(8,128)} %bitcast.9, f32[2,1152]{1,0:T(2,128)} %speed_hbm.1, ...), custom_call_target="tpu_custom_call" | custom-call | tf_op jit(solution)/shard_map/wave_step/pallas_call | solution.py:594
  76.2 0.0 copy-done
  76.2 0.0 copy-done.1
  76.2 2.0 %ocean_step.1 = (f32[448,1152]{1,0:T(8,128)}, f32[2,40,256]{2,1,0:T(8,128)}) custom-call(f32[896,128]{1,0:T(8,128)S(1)} %get-tuple-element.7.profiles, f32[448,1152]{1,0:T(8,128)S(1)} %get-tuple-element.8.waves, f32[40,256]{1,0:T(8,128)S(1)} %get-tuple-element.9.zeta, f32[1,256]{1,0:T(1,128)S(1)} %copy-done.1, f32[2,40,256]{2,1,0:T(8,128)S(1)} %bitcast.10), custom_call_target="tpu_custom_call" | custom-call | tf_op jit(solution)/shard_map/ocean_step/pallas_call | solution.py:668
Async XLA Ops:
  0.6 75.6 %copy-start = (f32[1,2,40,256]{3,2,1,0:T(8,128)S(1)}, f32[1,2,40,256]{3,2,1,0:T(8,128)}, u32[]{:S(2)}) copy-start(f32[1,2,40,256]{3,2,1,0:T(8,128)} %param.19) | copy-start | bytes 245764
  0.6 75.6 %copy-start.1 = (f32[1,256]{1,0:T(1,128)S(1)}, f32[1,256]{1,0:T(1,128)}, u32[]{:S(2)}) copy-start(f32[1,256]{1,0:T(1,128)} %coriolis.1) | copy-start | bytes 3076

commit v6 on v5

--- a/solution.py
+++ b/solution.py
@@ -109,6 +109,11 @@
     def load_inter(k):
         return pltpu.make_async_copy(inter_hbm.at[:, lanes(k)], inter.at[k], load_sem.at[1, k])
 
+    @pl.loop(0, chunks)
+    def _(k):
+        load_spec(k).start()
+
+    load_inter(0).start()
     barrier = pltpu.get_barrier_semaphore()
 
     @pl.loop(1, tiles)
@@ -119,11 +124,7 @@
 
     pl.semaphore_signal(barrier, inc=1, device_id={"grid": 1 - grid}, device_id_type=MESH)
 
-    @pl.loop(0, chunks)
-    def _(k):
-        load_spec(k).start()
-
-    @pl.loop(0, chunks)
+    @pl.loop(1, chunks)
     def _(k):
         load_inter(k).start()
 
@@ -308,6 +309,23 @@
 
         zeta[...] = taken(velocity[1], apart(0, 1)) - taken(velocity[0], apart(2, 3))
 
+    def set_out(k):
+        pos = jnp.broadcast_to(speed[1:2, lanes(k)] > 0.0, (rows, LANES))
+        for q in range(SIDE):
+            wide[k, pl.ds(SIDE * SUB + SIDE + q, rows, stride=SUB), :] = jnp.where(
+                pos, own[k, q], own[k, SIDE - 1 - q]
+            )
+        outside = pl.multiple_of((rows + SIDE) * SUB * grid, SUB)
+        wide[k, pl.ds(outside, SIDE * SUB), :] = jnp.zeros((SIDE * SUB, LANES), f32)
+        turn = turned(k, ring)
+        each = jnp.broadcast_to(speed[1:2, lanes(k)], (SUB, LANES)) > 0.0
+
+        @pl.loop(0, tall // SUB)
+        def _(part):
+            for u in range(SUB):
+                at = pl.ds(pl.multiple_of((part * SUB + u) * SUB, SUB), SUB)
+                mask_now[at, :] = jnp.where(each, mask_pos[turn, at, :], mask_neg[turn, at, :])
+
     def assemble(k):
         pos = jnp.broadcast_to(speed[1:2, lanes(k)] > 0.0, (rows, LANES))
         from_left = block(k) > 0
@@ -316,54 +334,45 @@
             lower = jnp.where(from_left, left[k, s], 0.0)
             upper = jnp.where(from_right, right[k, SIDE - 1 - s], 0.0)
             wide[k, pl.ds(SIDE * SUB + s, rows, stride=SUB), :] = jnp.where(pos, lower, upper)
-        for q in range(SIDE):
-            wide[k, pl.ds(SIDE * SUB + SIDE + q, rows, stride=SUB), :] = jnp.where(
-                pos, own[k, q], own[k, SIDE - 1 - q]
-            )
-        outside = pl.multiple_of((rows + SIDE) * SUB * grid, SUB)
-        wide[k, pl.ds(outside, SIDE * SUB), :] = jnp.zeros((SIDE * SUB, LANES), f32)
 
     def sweep(k):
         spread = lambda v: jnp.broadcast_to(v, (SUB, LANES))
         cx = speed[0:1, lanes(k)]
         cy = speed[1:2, lanes(k)]
-        down_rate = spread(jnp.maximum(cx, 0.0))
-        up_rate = spread(jnp.maximum(-cx, 0.0))
+        along = jnp.where(grid == 0, cx, -cx)
+        behind_rate = spread(jnp.maximum(along, 0.0))
+        front_rate = spread(jnp.maximum(-along, 0.0))
         side_rate = spread(jnp.abs(cy))
-        keep = 1.0 - down_rate - up_rate - side_rate
-        pos = spread(cy) > 0.0
-        turn = turned(k, ring)
-
-        @pl.loop(0, tall // SUB)
-        def _(part):
-            for u in range(SUB):
-                at = pl.ds(pl.multiple_of((part * SUB + u) * SUB, SUB), SUB)
-                mask_now[at, :] = jnp.where(pos, mask_pos[turn, at, :], mask_neg[turn, at, :])
-
+        keep = 1.0 - behind_rate - front_rate - side_rate
         zero = jnp.zeros((SUB, LANES), f32)
 
         def part(i, carry):
             held_rows = [list(pair) for pair in carry[0]]
             masks = list(carry[1])
             for u in range(SUB):
-                at = pl.ds(pl.multiple_of((i * SUB + u) * SUB, SUB), SUB)
+                r = i * SUB + u
+                row = r + grid * (tall - 1 - 2 * r)
+                at = pl.ds(pl.multiple_of(row * SUB, SUB), SUB)
+                to = pl.ds(pl.multiple_of((row + grid * SUB) * SUB, SUB), SUB)
                 value = wide[k, at, :]
                 for stage in range(SIDE):
                     previous, current = held_rows[stage]
                     moved = (
                         keep * current
-                        + down_rate * previous
-                        + up_rate * value
+                        + behind_rate * previous
+                        + front_rate * value
                         + side_rate * pltpu.roll(current, 1, 0)
                     )
                     held_rows[stage] = [current, value]
                     value = moved * masks[stage]
-                swept[at, :] = value
+                swept[to, :] = value
                 masks = [mask_now[at, :]] + masks[: SIDE - 1]
             return tuple(tuple(pair) for pair in held_rows), tuple(masks)
 
         start = (tuple((zero, zero) for _ in range(SIDE)), (zero,) * SIDE)
-        lax.fori_loop(0, tall // SUB, part, start)
+        nearly = lax.fori_loop(0, tall // SUB - 1, part, start)
+        send_edge(k).wait_recv()
+        part(tall // SUB - 1, nearly)
         wanted = jnp.broadcast_to(cy > 0.0, (rows, LANES))
         columns = [
             swept[pl.ds(2 * SIDE * SUB + SIDE + q, rows, stride=SUB), :] for q in range(SIDE)
@@ -434,6 +443,8 @@
         def _():
             prepare_zeta()
 
+        set_out(t)
+
         @pl.when(t < early)
         def _():
             for side in range(2):
@@ -448,12 +459,12 @@
         assemble(t)
         send_edge(t).start()
 
+        sweep(t)
+
         @pl.when(t >= 2)
         def _():
             finish(t - 2)
 
-        send_edge(t).wait_recv()
-        sweep(t)
 
     @pl.loop(chunks - 2, chunks)
     def _(k):
@@ -463,7 +474,7 @@
     both = jnp.concatenate(split(stokes[...]), axis=1)
     lane = lax.broadcasted_iota(jnp.int32, (per, LANES), 1)
     for step in range(parts):
-        part = lax.rem(place // per + step, parts)
+        part = lax.rem(place // per + (2, 1, 3, 0)[step], parts)
         term = jnp.dot(
             placer[pl.ds(pl.multiple_of(part * per * slots, 2 * SUB), per * slots), :],
             both,
@@ -482,7 +493,7 @@
         for row, values in enumerate(packed):
             posted[pl.ds(part * per, per), row, :] = values
 
-        @pl.loop(1 if step == 0 else 0, per)
+        @pl.loop(1 if step == parts - 1 else 0, per)
         def _(d):
             post(part * per + lax.rem(place + d, per)).start()
 
@@ -616,7 +627,7 @@
             piece,
             piece,
             pltpu.VMEM((chunks, tall * SUB, LANES), f32),
-            mask,
+            pltpu.VMEM(((tall + SUB) * SUB, LANES), f32),
             piece,
             piece,
             pltpu.VMEM((chunks, held, LANES), f32),

time: 78.6 us -> 78.6 us (level)
  no operation moved by 1% of the time
where the time goes in v6:
time: 78.6 us; the launch traced here: 78.1 us
  Pallas kernels  77.5 us (99%)
    pallas_call x1, Pallas kernels, per_device(): pl.pallas_call(wave_kernel, out_shape=(jax.ShapeDtypeStruct((held, comps)...  75.5 us
    pallas_call x1, Pallas kernels, per_device(): pl.pallas_call(ocean_kernel, out_shape=(jax.ShapeDtypeStruct((held, comps...  1.98 us

profile of v6, /device:TPU:0, one launch (start us, length us, event | category | flops | bytes accessed | tf_op | source)
XLA Modules:
  0.0 78.1 jit_solution(14228815323707189258)
XLA Ops:
  0.6 0.0 copy-start
  0.6 0.0 copy-start.1
  0.7 75.5 %wave_step.1 = (f32[448,1152]{1,0:T(8,128)S(1)}, f32[896,128]{1,0:T(8,128)S(1)}, f32[40,256]{1,0:T(8,128)S(1)}) custom-call(f32[448,1152]{1,0:T(8,128)} %bitcast.11, bf16[1152,1152]{1,0:T(8,128)(2,1)} %inter_hbm.1, s32[2,28672]{1,0:T(2,128)} %sea_hbm.1, f32[80,1152]{1,0:T(8,128)} %bitcast.12, f32[2,40,256]{2,1,0:T(8,128)} %bitcast.9, f32[2,1152]{1,0:T(2,128)} %speed_hbm.1, ...), custom_call_target="tpu_custom_call" | custom-call | tf_op jit(solution)/shard_map/wave_step/pallas_call | solution.py:605
  76.1 0.0 copy-done
  76.2 0.0 copy-done.1
  76.2 2.0 %ocean_step.1 = (f32[448,1152]{1,0:T(8,128)}, f32[2,40,256]{2,1,0:T(8,128)}) custom-call(f32[896,128]{1,0:T(8,128)S(1)} %get-tuple-element.7.profiles, f32[448,1152]{1,0:T(8,128)S(1)} %get-tuple-element.8.waves, f32[40,256]{1,0:T(8,128)S(1)} %get-tuple-element.9.zeta, f32[1,256]{1,0:T(1,128)S(1)} %copy-done.1, f32[2,40,256]{2,1,0:T(8,128)S(1)} %bitcast.10), custom_call_target="tpu_custom_call" | custom-call | tf_op jit(solution)/shard_map/ocean_step/pallas_call | solution.py:679
Async XLA Ops:
  0.6 75.5 %copy-start = (f32[1,2,40,256]{3,2,1,0:T(8,128)S(1)}, f32[1,2,40,256]{3,2,1,0:T(8,128)}, u32[]{:S(2)}) copy-start(f32[1,2,40,256]{3,2,1,0:T(8,128)} %param.19) | copy-start | bytes 245764
  0.6 75.5 %copy-start.1 = (f32[1,256]{1,0:T(1,128)S(1)}, f32[1,256]{1,0:T(1,128)}, u32[]{:S(2)}) copy-start(f32[1,256]{1,0:T(1,128)} %coriolis.1) | copy-start | bytes 3076

commit v7 on v6

--- a/solution.py
+++ b/solution.py
@@ -493,8 +493,7 @@
         for row, values in enumerate(packed):
             posted[pl.ds(part * per, per), row, :] = values
 
-        @pl.loop(1 if step == parts - 1 else 0, per)
-        def _(d):
+        for d in range(1 if step == parts - 1 else 0, per):
             post(part * per + lax.rem(place + d, per)).start()
 
     arrived[place] = posted[place]

time: 78.6 us -> 78.4 us (level)
  no operation moved by 1% of the time
where the time goes in v7:
time: 78.4 us; the launch traced here: 78.3 us
  Pallas kernels  77.6 us (99%)
    pallas_call x1, Pallas kernels, per_device(): pl.pallas_call(wave_kernel, out_shape=(jax.ShapeDtypeStruct((held, comps)...  75.6 us
    pallas_call x1, Pallas kernels, per_device(): pl.pallas_call(ocean_kernel, out_shape=(jax.ShapeDtypeStruct((held, comps...  1.98 us

profile of v7, /device:TPU:0, one launch (start us, length us, event | category | flops | bytes accessed | tf_op | source)
XLA Modules:
  0.0 78.3 jit_solution(614077603870614870)
XLA Ops:
  0.6 0.0 copy-start
  0.6 0.0 copy-start.1
  0.7 75.6 %wave_step.1 = (f32[448,1152]{1,0:T(8,128)S(1)}, f32[896,128]{1,0:T(8,128)S(1)}, f32[40,256]{1,0:T(8,128)S(1)}) custom-call(f32[448,1152]{1,0:T(8,128)} %bitcast.11, bf16[1152,1152]{1,0:T(8,128)(2,1)} %inter_hbm.1, s32[2,28672]{1,0:T(2,128)} %sea_hbm.1, f32[80,1152]{1,0:T(8,128)} %bitcast.12, f32[2,40,256]{2,1,0:T(8,128)} %bitcast.9, f32[2,1152]{1,0:T(2,128)} %speed_hbm.1, ...), custom_call_target="tpu_custom_call" | custom-call | tf_op jit(solution)/shard_map/wave_step/pallas_call | solution.py:604
  76.3 0.0 copy-done
  76.3 0.0 copy-done.1
  76.3 2.0 %ocean_step.1 = (f32[448,1152]{1,0:T(8,128)}, f32[2,40,256]{2,1,0:T(8,128)}) custom-call(f32[896,128]{1,0:T(8,128)S(1)} %get-tuple-element.7.profiles, f32[448,1152]{1,0:T(8,128)S(1)} %get-tuple-element.8.waves, f32[40,256]{1,0:T(8,128)S(1)} %get-tuple-element.9.zeta, f32[1,256]{1,0:T(1,128)S(1)} %copy-done.1, f32[2,40,256]{2,1,0:T(8,128)S(1)} %bitcast.10), custom_call_target="tpu_custom_call" | custom-call | tf_op jit(solution)/shard_map/ocean_step/pallas_call | solution.py:678
Async XLA Ops:
  0.6 75.6 %copy-start = (f32[1,2,40,256]{3,2,1,0:T(8,128)S(1)}, f32[1,2,40,256]{3,2,1,0:T(8,128)}, u32[]{:S(2)}) copy-start(f32[1,2,40,256]{3,2,1,0:T(8,128)} %param.19) | copy-start | bytes 245764
  0.6 75.6 %copy-start.1 = (f32[1,256]{1,0:T(1,128)S(1)}, f32[1,256]{1,0:T(1,128)}, u32[]{:S(2)}) copy-start(f32[1,256]{1,0:T(1,128)} %coriolis.1) | copy-start | bytes 3076
